TPU v7x, 32 devices: a whole 2x2x4 slice. The times are simulated.
32 devices in a mesh: blk: 8 (over y, x, core), lines: 4 (over z).
Axes of the slice: x: 2, y: 2, z: 4, core: 2. Of those that a mesh axis runs over, the one named last changes fastest.
Arguments:
- velocity: float32 [3, 12288, 1024], P(None, 'lines', 'blk'), may hold values from -6 to 6
- metric: float32 [1024], P('blk'), may hold values from 0.5 to 2
Outputs:
- derivs: float32 [3, 12288, 1024], P(None, 'lines', 'blk')
- profile: float32 [1024], P('blk')
All inputs are finite; a program needn't handle non-finite values.
Results may differ from a plain program's by a relative error of at most 0.00007.
Values sent between devices are 32-bit elements; how exact they have to be, the bound alone decides.
No kernel may reach another device: no remote copies, remote signals or barrier semaphores. Data moves between devices by JAX's collectives and lax.ppermute only.
A program may use at most 128 MiB of HBM per device.

v0:
```python
import jax
import jax.numpy as jnp
from jax import lax
from jax.sharding import PartitionSpec as P

ALPHA = 1.0 / 3.0
COEF_A = 7.0 / 9.0
COEF_B = 1.0 / 36.0


def block_inverse(width):
    counter = jnp.arange(width, dtype=jnp.int32) + 1
    product = counter[:, None] * counter[None, :] % (2 * (width + 1))
    angles = jnp.pi / (width + 1.0)
    sines = jnp.sqrt(2.0 / (width + 1.0)) * jnp.sin(angles * product.astype(jnp.float32))
    eigen = 1.0 + 2.0 * ALPHA * jnp.cos(angles * counter.astype(jnp.float32))
    return jnp.dot(sines / eigen[None, :], sines, precision=lax.Precision.HIGHEST)


def solve_rows(source, inverse):
    shape = source.shape
    flat = jnp.dot(source.reshape(-1, shape[-1]), inverse, precision=lax.Precision.HIGHEST)
    return flat.reshape(shape)


def interface(first_own, last_own, last_left, first_right, couple):
    factor = 1.0 / (1.0 - couple * couple)
    last_prev = (last_left - couple * first_own) * factor
    last_here = (last_own - couple * first_right) * factor
    first_next = first_right - couple * last_here
    return (last_prev, first_next)


def correct(partial_value, inverse, last_prev, first_next):
    width = inverse.shape[0]
    return partial_value - ALPHA * (
        last_prev[..., None] * inverse[:, 0] + first_next[..., None] * inverse[:, width - 1]
    )


def local(velocity, metric):
    width = velocity.shape[2]
    inverse = block_inverse(width)
    couple = ALPHA * inverse[0, 0]
    lines_block = lax.all_to_all(velocity, "blk", split_axis=1, concat_axis=2, tiled=True)
    count = lines_block.shape[-1]
    source = COEF_A * (jnp.roll(lines_block, -1, -1) - jnp.roll(lines_block, 1, -1)) + COEF_B * (
        jnp.roll(lines_block, -2, -1) - jnp.roll(lines_block, 2, -1)
    )
    blocks = source.reshape(lines_block.shape[0], lines_block.shape[1], count // width, width)
    partial_value = solve_rows(blocks, inverse)
    first_own = partial_value[..., 0]
    last_own = partial_value[..., width - 1]
    last_prev, first_next = interface(
        first_own, last_own, jnp.roll(last_own, 1, 2), jnp.roll(first_own, -1, 2), couple
    )
    whole = correct(partial_value, inverse, last_prev, first_next).reshape(lines_block.shape)
    solved = lax.all_to_all(whole, "blk", split_axis=2, concat_axis=1, tiled=True)
    derivs = solved * metric
    squares = jnp.sum(derivs * derivs, axis=(0, 1))
    total = lax.psum(squares, "lines")
    profile = total / (velocity.shape[1] * lax.axis_size("lines"))
    return (derivs, profile)


def solution(mesh):
    in_specs = (P(None, "lines", "blk"), P("blk"))
    out_specs = (P(None, "lines", "blk"), P("blk"))
    return jax.shard_map(local, mesh=mesh, in_specs=in_specs, out_specs=out_specs, check_vma=False)
```

profile of v0, /device:TPU:0, one launch (start us, length us, event | category | flops | bytes accessed | tf_op | source)
XLA Modules:
  0.0 224.0 jit_solution(313442755634897913)
XLA Ops:
  0.6 8.7 %copy.19 = f32[3,3072,128]{2,0,1:T(4,128)} copy(f32[3,3072,128]{2,1,0:T(8,128)} %param.2) | data formatting | bytes 9437184 | tf_op args[0]
  9.3 5.2 %all-to-all-start = ((f32[3,3072,128]{2,0,1:T(4,128)}), f32[3,3072,128]{2,0,1:T(4,128)}, u32[]{:S(2)}, u32[]{:S(2)}) async-start(f32[3,3072,128]{2,0,1:T(4,128)} %copy.19), calls=%async_computation | async-start | bytes 12582912 | tf_op jit(solution)/shard_map/all_to_all | solution.py:45
  14.6 0.9 fusion.3
  15.4 0.5 slice.91
  17.9 68.4 %all-to-all-done = f32[3,3072,128]{2,0,1:T(4,128)} async-done(((f32[3,3072,128]{2,0,1:T(4,128)}), f32[3,3072,128]{2,0,1:T(4,128)}, u32[]{:S(2)}, u32[]{:S(2)}) %all-to-all-start) | async-done | bytes 4718624 | tf_op jit(solution)/shard_map/all_to_all | solution.py:45
  86.3 5.3 %copy.20 = f32[3,3072,128]{2,1,0:T(8,128)} copy(f32[3,3072,128]{2,0,1:T(4,128)} %all-to-all-done) | data formatting | bytes 9437184 | tf_op jit(solution)/shard_map/all_to_all | solution.py:45
  91.6 6.1 %copy.21 = f32[3,384,8,128]{1,3,2,0:T(8,128)} copy(f32[3,384,8,128]{3,1,2,0:T(8,128)} %bitcast.50) | data formatting | bytes 9437184 | tf_op jit(solution)/shard_map/all_to_all | solution.py:45
  97.7 0.0 copy-start
  97.7 4.5 %fusion.33 = (f32[3,384,1023]{1,2,0:T(8,128)S(1)}, f32[3,384,1023]{1,2,0:T(8,128)S(1)}) fusion(f32[3,384,1024]{1,2,0:T(8,128)} %bitcast.42), kind=kLoop, calls=%fused_computation.53 | loop fusion | bytes 18855936 | tf_op jit(solution)/shard_map/jit(_roll_static)/slice | solution.py:47
  102.2 0.6 copy-done
  102.8 2.8 %fusion.31 = (f32[3,384,1022]{1,2,0:T(8,128)S(1)}, f32[3,384,1022]{1,2,0:T(8,128)}) fusion(f32[3,384,1024]{1,2,0:T(8,128)S(1)} %bitcast.43), kind=kLoop, calls=%fused_computation.51 | loop fusion | bytes 18837504 | tf_op jit(solution)/shard_map/jit(_roll_static)/slice | solution.py:48
  105.6 6.7 %fusion.1 = f32[3,384,1024]{1,2,0:T(8,128)S(1)} fusion(f32[3,384,1]{1,2,0:T(1,128)S(1)} %get-tuple-element.9, f32[3,384,1023]{1,2,0:T(8,128)S(1)} %get-tuple-element.11, f32[3,384,1023]{1,2,0:T(8,128)S(1)} %get-tuple-element.10, f32[3,384,1]{1,2,0:T(1,128)S(1)} %get-tuple-element.8, f32[3,384,2]{1,2,0:T(2,128)S(1)} %get-tuple-element.5, ...), kind=kLoop, calls=%fused_computation.3 | loop fusion | flops 10616832 | bytes 23592960 | tf_op jit(solution)/shard_map/add | solution.py:47
  112.3 4.7 %fusion.10 = f32[3,384,8,128]{1,3,2,0:T(8,128)S(1)} fusion(f32[3,384,8,128]{1,3,2,0:T(8,128)S(1)} %bitcast.48, f32[128,128]{0,1:T(8,128)S(1)} %fusion.3), kind=kOutput, calls=%fused_computation.15 | convolution fusion | flops 1811939328 | bytes 9502720 | tf_op jit(solution)/shard_map/dot_general | solution.py:22
  117.1 0.1 fusion.29
  117.3 1.0 multiply_subtract_fusion
  118.3 3.2 %copy.26 = f32[3,384,1024]{1,0,2:T(4,128)S(1)} copy(f32[3,384,1024]{1,2,0:T(8,128)S(1)} %bitcast.49) | data formatting | bytes 9437184 | tf_op jit(solution)/shard_map/reshape | solution.py:57
  121.5 74.9 %all_to_all.36 = f32[3,384,1024]{1,0,2:T(4,128)} all-to-all(f32[3,384,1024]{1,0,2:T(4,128)S(1)} %copy.26), channel_id=1, replica_groups=mesh['blk'=8,'lines'=4] {'blk'}, dimensions={2} | all-to-all | bytes 9437184 | tf_op jit(solution)/shard_map/all_to_all | solution.py:58
  196.4 6.9 %copy.27 = f32[3,8,384,128]{3,2,1,0:T(8,128)} copy(f32[3,8,384,128]{2,0,3,1:T(4,128)} %bitcast.46) | data formatting | bytes 9437184 | tf_op jit(solution)/shard_map/all_to_all | solution.py:58
  203.3 0.0 copy-done.2
  203.3 4.9 %multiply_reduce_fusion = f32[128]{0:T(128)S(1)} fusion(f32[3,8,384,128]{2,0,3,1:T(4,128)} %bitcast.47, f32[128]{0:T(128)S(1)} %copy-done.2), kind=kLoop, calls=%fused_computation | loop fusion | flops 3538816 | bytes 4719616 | tf_op jit(solution)/shard_map/reduce_sum | solution.py:60
  208.3 0.0 copy-done.1
  208.3 2.5 %bitcast_multiply_fusion = f32[3,3072,128]{2,1,0:T(8,128)} fusion(f32[3,8,384,128]{3,2,1,0:T(8,128)S(1)} %copy-done.1, f32[128]{0:T(128)S(1)} %copy-done.2), kind=kLoop, calls=%fused_computation.6 | loop fusion | flops 1179648 | bytes 9437696 | tf_op jit(solution)/shard_map/mul | solution.py:59
  210.8 12.7 %psum.7 = f32[128]{0:T(128)S(1)} all-reduce(f32[128]{0:T(128)S(1)} %multiply_reduce_fusion), channel_id=1, replica_groups=mesh['blk'=8,'lines'=4] {'lines'}, use_global_device_ids=true, to_apply=%region_1.2 | all-reduce | flops 128 | bytes 1024 | tf_op jit(solution)/shard_map/psum | solution.py:61
  223.5 0.5 broadcast_multiply_fusion
  (14 shorter events, 0.1 us)
Async XLA Ops:
  9.3 77.0 %all-to-all-start = ((f32[3,3072,128]{2,0,1:T(4,128)}), f32[3,3072,128]{2,0,1:T(4,128)}, u32[]{:S(2)}, u32[]{:S(2)}) async-start(f32[3,3072,128]{2,0,1:T(4,128)} %copy.19), calls=%async_computation | async-start | bytes 12582912 | tf_op jit(solution)/shard_map/all_to_all | solution.py:45
  97.7 5.1 %copy-start = (f32[3,384,8,128]{1,3,2,0:T(8,128)S(1)}, f32[3,384,8,128]{1,3,2,0:T(8,128)}, u32[]{:S(2)}) copy-start(f32[3,384,8,128]{1,3,2,0:T(8,128)} %copy.21) | copy-start | bytes 14155780
  196.4 6.9 %copy-start.2 = (f32[128]{0:T(128)S(1)}, f32[128]{0:T(128)}, u32[]{:S(2)}) copy-start(f32[128]{0:T(128)} %param.3) | copy-start | bytes 1540
  203.3 5.0 %copy-start.1 = (f32[3,8,384,128]{3,2,1,0:T(8,128)S(1)}, f32[3,8,384,128]{3,2,1,0:T(8,128)}, u32[]{:S(2)}) copy-start(f32[3,8,384,128]{3,2,1,0:T(8,128)} %copy.27) | copy-start | bytes 14155780
where the time goes:
time: 225 us; the launch traced here: 224 us
  blocking collectives  87.6 us (39%)
  waiting for transfers between devices  68.4 us (30%)
  local copies, waits for them, and re-layouts  38.7 us (17%)
  other arithmetic  15.8 us (7%)
  matrix products  5.58 us (2%)
  starting transfers between devices  5.17 us (2%)
  between operations  2.74 us (1%)
    all_to_all x1, blocking collectives, local(): lax.all_to_all(whole, 'blk', split_axis=2, concat_axis=1, tiled=True)  74.9 us
    all_to_all x1, waiting for transfers between devices, local(): lax.all_to_all(velocity, 'blk', split_axis=1, concat_axis=2, tiled=True)  68.4 us
    psum x1, blocking collectives, local(): total = lax.psum(squares, 'lines')  12.7 us
    all_to_all x2, local copies, waits for them, and re-layouts, local(): lax.all_to_all(velocity, 'blk', split_axis=1, concat_axis=2, tiled=True)  11.3 us
    unnamed x8, local copies, waits for them, and re-layouts  9.3 us
    all_to_all x1, local copies, waits for them, and re-layouts, local(): lax.all_to_all(whole, 'blk', split_axis=2, concat_axis=1, tiled=True)  6.91 us
    add x1, other arithmetic, local(): COEF_A * (jnp.roll(lines_block, -1, -1) - jnp.roll(lines_block, 1, -1))  6.72 us
    all_to_all x1, starting transfers between devices, local(): lax.all_to_all(velocity, 'blk', split_axis=1, concat_axis=2, tiled=True)  5.17 us
  transfers between devices with their start and end apart: 1, of which 1 were waited for; matrix products, arithmetic and copies ran while one was open for 1% of the time, Pallas kernels for 0%

commit v1 on v0

v1 whole, which is shorter than its diff:
```python
import functools

import jax
import jax.numpy as jnp
import ml_dtypes
import numpy as np
from jax import lax
from jax.experimental import pallas as pl
from jax.experimental.pallas import tpu as pltpu
from jax.sharding import PartitionSpec as P

ALPHA = 1.0 / 3.0
COEF_A = 7.0 / 9.0
COEF_B = 1.0 / 36.0

ROOT = np.sqrt(1.0 - 4.0 * ALPHA * ALPHA)
RATIO = (1.0 - ROOT) / (2.0 * ALPHA)
NEAR = COEF_B / ALPHA
GAIN = (COEF_A - NEAR) / ROOT * (1.0 / RATIO - RATIO)

WIDTH = 128
HALF = WIDTH // 2
CHUNKS = 32
LIMIT = 24 * 2**20


def powers(exponents):
    return (-RATIO) ** np.asarray(exponents, np.float64)


def split(matrix):
    high = matrix.astype(np.float32).astype(ml_dtypes.bfloat16)
    low = (matrix - high.astype(np.float64)).astype(np.float32).astype(ml_dtypes.bfloat16)
    return high, low


def local_weights():
    lag = np.arange(WIDTH)[None, :] - np.arange(WIDTH)[:, None]
    weights = np.sign(lag) * (GAIN * powers(np.abs(lag)) - NEAR * (np.abs(lag) == 1))
    both = np.concatenate(split(weights), axis=1)
    return np.concatenate([both, both], axis=0)


def edge_weights():
    station = np.arange(WIDTH)
    columns = [powers(station), station == 0, powers(WIDTH - 1 - station), station == WIDTH - 1]
    weights = np.zeros((WIDTH, WIDTH))
    for lane in range(WIDTH):
        weights[:, lane] = columns[2 * (lane // HALF) + lane % 2]
    both = np.concatenate(split(weights), axis=1)
    return np.concatenate([both, both], axis=0)


def reach_weights():
    station = np.arange(WIDTH)
    rows = [GAIN * powers(station + 1), -NEAR * (station == 0), -GAIN * powers(WIDTH - station), NEAR * (station == WIDTH - 1)]
    weights = np.zeros((WIDTH, 2 * WIDTH))
    for lane in range(WIDTH):
        start = WIDTH * (lane % 4 // 2)
        weights[lane, start : start + WIDTH] = rows[2 * (lane // HALF) + lane % 2]
    return np.concatenate(split(weights), axis=0)


def parity():
    return lax.rem(lax.axis_index("blk"), 2)


def edges_kernel(groups, velocity_ref, weights_ref, split_ref, outer_ref, inner_ref, buffer, packed, sems):
    rows = velocity_ref.shape[0]
    span, count = rows // groups, rows // CHUNKS
    copies = []
    for g in range(groups):
        part = pl.ds(g * span, span)
        copies.append(pltpu.make_async_copy(velocity_ref.at[part], buffer.at[part], sems.at[g]))
        copies[-1].start()
    weights = weights_ref[...]
    owner = lax.broadcasted_iota(jnp.int32, (count, WIDTH), 1) % HALF // 2
    per = CHUNKS // groups
    for g in range(groups):
        copies[g].wait()
        for c in range(g * per, (g + 1) * per):
            part = pl.ds(c * count, count)
            value = buffer[part, :]
            high = value.astype(jnp.bfloat16)
            low = (value - high.astype(jnp.float32)).astype(jnp.bfloat16)
            both = jnp.concatenate([high, low], axis=1)
            split_ref[part, :] = both
            out = jnp.dot(both, weights, preferred_element_type=jnp.float32)
            pltpu.store(packed, out[:, :WIDTH] + out[:, WIDTH:], mask=owner == c)
    lower = packed[: count // 2, :]
    upper = packed[count // 2 :, :]
    lane = lax.broadcasted_iota(jnp.int32, lower.shape, 1)
    first = jnp.where(lane < HALF, lower, pltpu.roll(upper, HALF, 1))
    last = jnp.where(lane < HALF, pltpu.roll(lower, HALF, 1), upper)
    even = parity() == 0
    outer_ref[...] = jnp.where(even, first, last)
    inner_ref[...] = jnp.where(even, last, first)


def local_kernel(steps, split_ref, weights_ref, out_ref):
    count = split_ref.shape[0] // steps
    weights = weights_ref[...]

    def step(s, carry):
        part = pl.ds(pl.multiple_of(s * count, count), count)
        out = jnp.dot(split_ref[part, :], weights, preferred_element_type=jnp.float32)
        out_ref[part, :] = out[:, :WIDTH] + out[:, WIDTH:]
        return carry

    lax.fori_loop(0, steps, step, 0)


def reach_kernel(solved_ref, outer_ref, inner_ref, weights_ref, metric_ref, out_ref, sums_ref):
    count = solved_ref.shape[0] // CHUNKS
    even = parity() == 0
    left = jnp.where(even, outer_ref[...], inner_ref[...])
    right = jnp.where(even, inner_ref[...], outer_ref[...])
    lane = lax.broadcasted_iota(jnp.int32, left.shape, 1)
    lower = jnp.where(lane < HALF, left, pltpu.roll(right, HALF, 1))
    upper = jnp.where(lane < HALF, pltpu.roll(left, HALF, 1), right)
    packed = jnp.concatenate([lower, upper], axis=0)
    slot = lax.broadcasted_iota(jnp.int32, packed.shape, 1) % HALF // 4
    high = packed.astype(jnp.bfloat16).astype(jnp.float32)
    low = packed - high
    low = jnp.where(slot % 2 == 0, pltpu.roll(low, WIDTH - 4, 1), pltpu.roll(low, 4, 1))
    high, low = high.astype(jnp.bfloat16), low.astype(jnp.bfloat16)
    slot = slot.astype(jnp.bfloat16)
    zero = jnp.zeros_like(high)
    weights = weights_ref[...]
    metric = jnp.broadcast_to(metric_ref[...], (count, WIDTH))
    sums = jnp.zeros((8, WIDTH), jnp.float32)
    for p in range(CHUNKS // 2):
        mine = jnp.where(slot == p, high, zero)
        rows = jnp.concatenate([jnp.where(slot == (p ^ 1), low, mine), mine], axis=1)
        out = jnp.dot(rows, weights, preferred_element_type=jnp.float32)
        for e in range(2):
            part = pl.ds((2 * p + e) * count, count)
            value = (solved_ref[part, :] + out[:, e * WIDTH : (e + 1) * WIDTH]) * metric
            out_ref[part, :] = value
            sums = sums + jnp.sum((value * value).reshape(count // 8, 8, WIDTH), axis=0)
    sums_ref[...] = jnp.sum(sums, axis=0, keepdims=True)


def local(velocity, metric):
    parts, lines, width = velocity.shape
    rows = parts * lines
    count = rows // CHUNKS
    blocks, across = lax.axis_size("blk"), lax.axis_size("lines")
    assert width == WIDTH and rows % (CHUNKS * 32) == 0 and blocks % 2 == 0
    vmem = pl.BlockSpec(memory_space=pltpu.VMEM)
    params = pltpu.CompilerParams(vmem_limit_bytes=LIMIT)
    f32 = jnp.float32
    groups = 8
    halves, outer, inner = pl.pallas_call(
        functools.partial(edges_kernel, groups),
        out_shape=(
            pltpu.VMEM((rows, 2 * width), jnp.bfloat16),
            pltpu.VMEM((count // 2, width), f32),
            pltpu.VMEM((count // 2, width), f32),
        ),
        in_specs=[pl.BlockSpec(memory_space=pl.ANY), vmem],
        out_specs=(vmem, vmem, vmem),
        scratch_shapes=[pltpu.VMEM((rows, width), f32), pltpu.VMEM((count, width), f32), pltpu.SemaphoreType.DMA((groups,))],
        compiler_params=params,
        name="edges",
    )(velocity.reshape(rows, width), jnp.asarray(edge_weights()))
    far = [(i, (i + 1) % blocks) for i in range(1, blocks, 2)]
    outer = lax.ppermute(outer, "blk", far + [(j, i) for i, j in far])
    inner = lax.ppermute(inner, "blk", [(i, i ^ 1) for i in range(blocks)])
    solved = pl.pallas_call(
        functools.partial(local_kernel, 4),
        out_shape=pltpu.VMEM((rows, width), f32),
        in_specs=[vmem, vmem],
        out_specs=vmem,
        compiler_params=params,
        name="local",
    )(halves, jnp.asarray(local_weights()))
    derivs, sums = pl.pallas_call(
        reach_kernel,
        out_shape=(pltpu.VMEM((rows, width), f32), pltpu.VMEM((1, width), f32)),
        in_specs=[vmem] * 5,
        out_specs=(vmem, vmem),
        compiler_params=params,
        name="reach",
    )(solved, outer, inner, jnp.asarray(reach_weights()), metric.reshape(1, width))
    if across & (across - 1) == 0:
        step = 1
        while step < across:
            sums = sums + lax.ppermute(sums, "lines", [(i, i ^ step) for i in range(across)])
            step *= 2
    else:
        sums = lax.psum(sums, "lines")
    profile = sums.reshape(width) / (lines * across)
    return derivs.reshape(velocity.shape), profile


def solution(mesh):
    in_specs = (P(None, "lines", "blk"), P("blk"))
    out_specs = (P(None, "lines", "blk"), P("blk"))
    return jax.shard_map(local, mesh=mesh, in_specs=in_specs, out_specs=out_specs, check_vma=False)
```

time: 225 us -> 24.8 us (0.11)
  blocking collectives: 87.6 us -> 0 us
  waiting for transfers between devices: 68.4 us -> 1.67 us
  local copies, waits for them, and re-layouts: 38.7 us -> 5.43 us
  other arithmetic: 15.8 us -> 0.52 us
  Pallas kernels: 0 us -> 6.8 us
  matrix products: 5.58 us -> 0 us
  starting transfers between devices: 5.17 us -> 9.5 us
    all_to_all x1 -> x0, blocking collectives: 74.9 us -> none  [local(): lax.all_to_all(whole, 'blk', split_axis=2, concat_axis=1, tiled=True)]
    all_to_all x1 -> x0, waiting for transfers between devices: 68.4 us -> none  [local(): lax.all_to_all(velocity, 'blk', split_axis=1, concat_axis=2, tiled=True)]
    all_to_all x3 -> x0, local copies, waits for them, and re-layouts: 18.2 us -> none  [the longest x2 11.3 us: local(): lax.all_to_all(velocity, 'blk', split_axis=1, concat_axis=2, tiled=True)]
    psum x1 -> x0, blocking collectives: 12.7 us -> none  [local(): total = lax.psum(squares, 'lines')]
    ppermute x0 -> x4, starting transfers between devices: none -> 9.5 us  [the longest x2 6.11 us: local(): lax.ppermute(sums, 'lines', [(i, i ^ step) for i in range(across)])]
    slice x6 -> x0, local copies, waits for them, and re-layouts: 7.91 us -> none  [the longest x2 4.52 us: local(): jnp.roll(lines_block, 1, -1)]
    pallas_call x0 -> x3, Pallas kernels: none -> 6.8 us  [the longest x1 3.77 us: local(): pl.pallas_call(functools.partial(edges_kernel, groups), out_shape=(pltpu....]
    add x3 -> x1, other arithmetic: 6.77 us -> 0.01 us  [local(): sums + lax.ppermute(sums, 'lines', [(i, i ^ step) for i in range(across)])]
  transfers between devices with their start and end apart: 1 -> 4, of which waited for: 1 -> 2; matrix products, arithmetic and copies ran while one was open for 1% -> 9% of each run, Pallas kernels for 0% -> 8%
where the time goes in v1:
time: 24.8 us; the launch traced here: 24.6 us
  starting transfers between devices  9.5 us (38%)
  Pallas kernels  6.8 us (27%)
  local copies, waits for them, and re-layouts  5.43 us (22%)
  waiting for transfers between devices  1.67 us (7%)
  between operations  0.67 us (3%)
  other arithmetic  0.52 us (2%)
    ppermute x2, starting transfers between devices, local(): lax.ppermute(sums, 'lines', [(i, i ^ step) for i in range(across)])  6.11 us
    unnamed x11, local copies, waits for them, and re-layouts  5.43 us
    pallas_call x1, Pallas kernels, local(): pl.pallas_call(functools.partial(edges_kernel, groups), out_shape=(pltpu....  3.77 us
    ppermute x1, starting transfers between devices, local(): outer = lax.ppermute(outer, 'blk', far + [(j, i) for i, j in far])  3.39 us
    pallas_call x1, Pallas kernels, local(): pl.pallas_call(functools.partial(local_kernel, 4), out_shape=pltpu.VMEM((...  1.87 us
    ppermute x2, waiting for transfers between devices, local(): lax.ppermute(sums, 'lines', [(i, i ^ step) for i in range(across)])  1.52 us
    pallas_call x1, Pallas kernels, local(): pl.pallas_call(reach_kernel, out_shape=(pltpu.VMEM((rows, width), f32), p...  1.16 us
    div x1, other arithmetic, local(): profile = sums.reshape(width) / (lines * across)  0.51 us
  transfers between devices with their start and end apart: 4, of which 2 were waited for; matrix products, arithmetic and copies ran while one was open for 9% of the time, Pallas kernels for 8%

profile of v1, /device:TPU:0, one launch (start us, length us, event | category | flops | bytes accessed | tf_op | source)
XLA Modules:
  0.0 24.6 jit_solution(17500972236343836104)
XLA Ops:
  0.6 0.0 copy-start
  0.6 2.3 %copy-done = f32[3,3072,128]{2,1,0:T(8,128)S(1)} copy-done((f32[3,3072,128]{2,1,0:T(8,128)S(1)}, f32[3,3072,128]{2,1,0:T(8,128)}, u32[]{:S(2)}) %copy-start) | copy-done | bytes 4718616
  3.0 0.0 copy-start.3
  3.0 0.9 %copy-done.3 = bf16[256,256]{1,0:T(8,128)(2,1)S(1)} copy-done((bf16[256,256]{1,0:T(8,128)(2,1)S(1)}, bf16[256,256]{1,0:T(8,128)(2,1)}, u32[]{:S(2)}) %copy-start.3) | copy-done | bytes 131096
  3.9 0.0 copy-start.1
  3.9 3.8 %edges.1 = (bf16[9216,256]{1,0:T(8,128)(2,1)S(1)}, f32[144,128]{1,0:T(8,128)S(1)}, f32[144,128]{1,0:T(8,128)S(1)}) custom-call(f32[9216,128]{1,0:T(8,128)S(1)} %bitcast.6, bf16[256,256]{1,0:T(8,128)(2,1)S(1)} %copy-done.3), custom_call_target="tpu_custom_call" | custom-call | tf_op jit(solution)/shard_map/edges/pallas_call | solution.py:154
  7.7 3.4 %collective-permute-start = (f32[144,128]{1,0:T(8,128)S(1)}, f32[144,128]{1,0:T(8,128)S(1)}, u32[]{:S(2)}, u32[]{:S(2)}) collective-permute-start(f32[144,128]{1,0:T(8,128)S(1)} %get-tuple-element.8), channel_id=1, source_target_pairs={{4,8},{12,16},{20,24},{28,0},{8,4},{16,12},{24,20},{0,28},{5,9},{1... | collective-permute-start | bytes 221192 | tf_op jit(solution)/shard_map/ppermute | solution.py:168
  11.0 0.0 collective-permute-start.1
  11.0 0.0 copy-done.1
  11.1 0.0 copy-start.2
  11.1 0.0 copy-start.4
  11.1 1.9 %local.1.solved_ref = f32[9216,128]{1,0:T(8,128)S(1)} custom-call(bf16[9216,256]{1,0:T(8,128)(2,1)S(1)} %get-tuple-element.7.split_ref, bf16[256,256]{1,0:T(8,128)(2,1)S(1)} %copy-done.1), custom_call_target="tpu_custom_call" | custom-call | tf_op jit(solution)/shard_map/local/pallas_call | solution.py:170
  12.9 0.1 collective-permute-done.outer_ref
  13.1 0.0 collective-permute-done.1.inner_ref
  13.1 0.0 copy-done.2
  13.1 0.0 copy-done.4
  13.1 1.2 %reach.1 = (f32[9216,128]{1,0:T(8,128)S(1)}, f32[1,128]{1,0:T(1,128)S(1)}) custom-call(f32[9216,128]{1,0:T(8,128)S(1)} %local.1.solved_ref, f32[144,128]{1,0:T(8,128)S(1)} %collective-permute-done.outer_ref, f32[144,128]{1,0:T(8,128)S(1)} %collective-permute-done.1.inner_ref, bf16[256,256]{1,0:T(8,128)(2,1)S(1)} %copy-done.2, f32[1,128]{1,0:T(1,128)S(1)} %bitcast.7), custom_call_target="tpu_custom_call" | custom-call | tf_op jit(solution)/shard_map/reach/pallas_call | solution.py:178
  14.3 3.1 %collective-permute-start.2 = (f32[1,128]{1,0:T(1,128)S(1)}, f32[1,128]{1,0:T(1,128)S(1)}, u32[]{:S(2)}, u32[]{:S(2)}) collective-permute-start(f32[1,128]{1,0:T(1,128)S(1)} %get-tuple-element.11), channel_id=1, source_target_pairs={{0,1},{1,0},{2,3},{3,2},{4,5},{5,4},{6,7},{7,6},{8,9},{9,8},{10,11... | collective-permute-start | bytes 1544 | tf_op jit(solution)/shard_map/ppermute | solution.py:189
  17.3 1.5 %collective-permute-done.2 = f32[1,128]{1,0:T(1,128)S(1)} collective-permute-done((f32[1,128]{1,0:T(1,128)S(1)}, f32[1,128]{1,0:T(1,128)S(1)}, u32[]{:S(2)}, u32[]{:S(2)}) %collective-permute-start.2) | collective-permute-done | bytes 544 | tf_op jit(solution)/shard_map/ppermute | solution.py:189
  18.9 3.0 %collective-permute-start.3 = (f32[1,128]{1,0:T(1,128)S(1)}, f32[1,128]{1,0:T(1,128)S(1)}, u32[]{:S(2)}, u32[]{:S(2)}) collective-permute-start(f32[1,128]{1,0:T(1,128)S(1)} %add.6), channel_id=1, source_target_pairs={{0,2},{1,3},{2,0},{3,1},{4,6},{5,7},{6,4},{7,5},{8,10},{9,11},{10,... | collective-permute-start | bytes 1544 | tf_op jit(solution)/shard_map/ppermute | solution.py:189
  21.9 2.2 %copy.7 = f32[3,3072,128]{2,1,0:T(8,128)} copy(f32[3,3072,128]{2,1,0:T(8,128)S(1)} %bitcast.5) | data formatting | bytes 9437184
  24.1 0.0 collective-permute-done.3
  24.1 0.5 %multiply_bitcast_fusion = f32[128]{0:T(128)} fusion(f32[1,128]{1,0:T(1,128)S(1)} %add.6, f32[1,128]{1,0:T(1,128)S(1)} %collective-permute-done.3), kind=kLoop, calls=%fused_computation | loop fusion | flops 256 | bytes 1536 | tf_op jit(solution)/shard_map/div | solution.py:193
  (1 shorter events, 0.0 us)
Async XLA Ops:
  0.6 2.3 %copy-start = (f32[3,3072,128]{2,1,0:T(8,128)S(1)}, f32[3,3072,128]{2,1,0:T(8,128)}, u32[]{:S(2)}) copy-start(f32[3,3072,128]{2,1,0:T(8,128)} %param.5) | copy-start | bytes 14155780
  3.0 0.9 %copy-start.3 = (bf16[256,256]{1,0:T(8,128)(2,1)S(1)}, bf16[256,256]{1,0:T(8,128)(2,1)}, u32[]{:S(2)}) copy-start(bf16[256,256]{1,0:T(8,128)(2,1)} %constant.9.clone.weights_ref) | copy-start | bytes 393220
  3.9 7.2 %copy-start.1 = (bf16[256,256]{1,0:T(8,128)(2,1)S(1)}, bf16[256,256]{1,0:T(8,128)(2,1)}, u32[]{:S(2)}) copy-start(bf16[256,256]{1,0:T(8,128)(2,1)} %constant.10.clone.weights_ref) | copy-start | bytes 393220
  7.7 5.4 %collective-permute-start = (f32[144,128]{1,0:T(8,128)S(1)}, f32[144,128]{1,0:T(8,128)S(1)}, u32[]{:S(2)}, u32[]{:S(2)}) collective-permute-start(f32[144,128]{1,0:T(8,128)S(1)} %get-tuple-element.8), channel_id=1, source_target_pairs={{4,8},{12,16},{20,24},{28,0},{8,4},{16,12},{24,20},{0,28},{5,9},{1... | collective-permute-start | bytes 221192 | tf_op jit(solution)/shard_map/ppermute | solution.py:168
  11.0 2.0 %collective-permute-start.1 = (f32[144,128]{1,0:T(8,128)S(1)}, f32[144,128]{1,0:T(8,128)S(1)}, u32[]{:S(2)}, u32[]{:S(2)}) collective-permute-start(f32[144,128]{1,0:T(8,128)S(1)} %get-tuple-element.9), channel_id=1, source_target_pairs={{0,4},{4,0},{8,12},{12,8},{16,20},{20,16},{24,28},{28,24},{1,5},{5... | collective-permute-start | bytes 221192 | tf_op jit(solution)/shard_map/ppermute | solution.py:169
  11.1 2.0 %copy-start.2 = (bf16[256,256]{1,0:T(8,128)(2,1)S(1)}, bf16[256,256]{1,0:T(8,128)(2,1)}, u32[]{:S(2)}) copy-start(bf16[256,256]{1,0:T(8,128)(2,1)} %constant.11.clone.weights_ref) | copy-start | bytes 393220
  11.1 2.0 %copy-start.4 = (f32[128]{0:T(128)S(1)}, f32[128]{0:T(128)}, u32[]{:S(2)}) copy-start(f32[128]{0:T(128)} %param.6) | copy-start | bytes 1540
  14.3 4.6 %collective-permute-start.2 = (f32[1,128]{1,0:T(1,128)S(1)}, f32[1,128]{1,0:T(1,128)S(1)}, u32[]{:S(2)}, u32[]{:S(2)}) collective-permute-start(f32[1,128]{1,0:T(1,128)S(1)} %get-tuple-element.11), channel_id=1, source_target_pairs={{0,1},{1,0},{2,3},{3,2},{4,5},{5,4},{6,7},{7,6},{8,9},{9,8},{10,11... | collective-permute-start | bytes 1544 | tf_op jit(solution)/shard_map/ppermute | solution.py:189
  18.9 5.2 %collective-permute-start.3 = (f32[1,128]{1,0:T(1,128)S(1)}, f32[1,128]{1,0:T(1,128)S(1)}, u32[]{:S(2)}, u32[]{:S(2)}) collective-permute-start(f32[1,128]{1,0:T(1,128)S(1)} %add.6), channel_id=1, source_target_pairs={{0,2},{1,3},{2,0},{3,1},{4,6},{5,7},{6,4},{7,5},{8,10},{9,11},{10,... | collective-permute-start | bytes 1544 | tf_op jit(solution)/shard_map/ppermute | solution.py:189

commit v2 on v1

--- a/solution.py
+++ b/solution.py
@@ -21,6 +21,7 @@
 WIDTH = 128
 HALF = WIDTH // 2
 CHUNKS = 32
+EARLY = 12
 LIMIT = 24 * 2**20
 
 
@@ -65,14 +66,17 @@
     return lax.rem(lax.axis_index("blk"), 2)
 
 
-def edges_kernel(groups, velocity_ref, weights_ref, split_ref, outer_ref, inner_ref, buffer, packed, sems):
+def edges_kernel(groups, velocity_ref, weights_hbm, split_ref, outer_ref, inner_ref, buffer, packed, weights_ref, sems):
     rows = velocity_ref.shape[0]
     span, count = rows // groups, rows // CHUNKS
+    fetch = pltpu.make_async_copy(weights_hbm, weights_ref, sems.at[groups])
+    fetch.start()
     copies = []
     for g in range(groups):
         part = pl.ds(g * span, span)
         copies.append(pltpu.make_async_copy(velocity_ref.at[part], buffer.at[part], sems.at[g]))
         copies[-1].start()
+    fetch.wait()
     weights = weights_ref[...]
     owner = lax.broadcasted_iota(jnp.int32, (count, WIDTH), 1) % HALF // 2
     per = CHUNKS // groups
@@ -110,7 +114,7 @@
     lax.fori_loop(0, steps, step, 0)
 
 
-def reach_kernel(solved_ref, outer_ref, inner_ref, weights_ref, metric_ref, out_ref, sums_ref):
+def reach_kernel(early, solved_ref, outer_ref, inner_ref, weights_ref, metric_ref, out_ref, rest_ref, sums_ref, buffer, sems):
     count = solved_ref.shape[0] // CHUNKS
     even = parity() == 0
     left = jnp.where(even, outer_ref[...], inner_ref[...])
@@ -129,6 +133,7 @@
     weights = weights_ref[...]
     metric = jnp.broadcast_to(metric_ref[...], (count, WIDTH))
     sums = jnp.zeros((8, WIDTH), jnp.float32)
+    copies = []
     for p in range(CHUNKS // 2):
         mine = jnp.where(slot == p, high, zero)
         rows = jnp.concatenate([jnp.where(slot == (p ^ 1), low, mine), mine], axis=1)
@@ -136,9 +141,24 @@
         for e in range(2):
             part = pl.ds((2 * p + e) * count, count)
             value = (solved_ref[part, :] + out[:, e * WIDTH : (e + 1) * WIDTH]) * metric
-            out_ref[part, :] = value
+            c = 2 * p + e
+            if c < early:
+                buffer[part, :] = value
+                copies.append(pltpu.make_async_copy(buffer.at[part], out_ref.at[part], sems.at[c]))
+                copies[-1].start()
+            else:
+                rest_ref[pl.ds((c - early) * count, count), :] = value
             sums = sums + jnp.sum((value * value).reshape(count // 8, 8, WIDTH), axis=0)
     sums_ref[...] = jnp.sum(sums, axis=0, keepdims=True)
+    for copy in copies:
+        copy.wait()
+
+
+def flush_kernel(early, rest_ref, derivs_ref, out_ref, sem):
+    rows = rest_ref.shape[0]
+    copy = pltpu.make_async_copy(rest_ref, out_ref.at[pl.ds(out_ref.shape[0] - rows, rows)], sem)
+    copy.start()
+    copy.wait()
 
 
 def local(velocity, metric):
@@ -148,6 +168,8 @@
     blocks, across = lax.axis_size("blk"), lax.axis_size("lines")
     assert width == WIDTH and rows % (CHUNKS * 32) == 0 and blocks % 2 == 0
     vmem = pl.BlockSpec(memory_space=pltpu.VMEM)
+    hbm = pl.BlockSpec(memory_space=pltpu.HBM)
+    in_hbm = functools.partial(pltpu.with_memory_space_constraint, memory_space=pltpu.HBM)
     params = pltpu.CompilerParams(vmem_limit_bytes=LIMIT)
     f32 = jnp.float32
     groups = 8
@@ -158,12 +180,17 @@
             pltpu.VMEM((count // 2, width), f32),
             pltpu.VMEM((count // 2, width), f32),
         ),
-        in_specs=[pl.BlockSpec(memory_space=pl.ANY), vmem],
+        in_specs=[hbm, hbm],
         out_specs=(vmem, vmem, vmem),
-        scratch_shapes=[pltpu.VMEM((rows, width), f32), pltpu.VMEM((count, width), f32), pltpu.SemaphoreType.DMA((groups,))],
+        scratch_shapes=[
+            pltpu.VMEM((rows, width), f32),
+            pltpu.VMEM((count, width), f32),
+            pltpu.VMEM((2 * width, 2 * width), jnp.bfloat16),
+            pltpu.SemaphoreType.DMA((groups + 1,)),
+        ],
         compiler_params=params,
         name="edges",
-    )(velocity.reshape(rows, width), jnp.asarray(edge_weights()))
+    )(in_hbm(velocity.reshape(rows, width)), in_hbm(jnp.asarray(edge_weights())))
     far = [(i, (i + 1) % blocks) for i in range(1, blocks, 2)]
     outer = lax.ppermute(outer, "blk", far + [(j, i) for i, j in far])
     inner = lax.ppermute(inner, "blk", [(i, i ^ 1) for i in range(blocks)])
@@ -175,14 +202,26 @@
         compiler_params=params,
         name="local",
     )(halves, jnp.asarray(local_weights()))
-    derivs, sums = pl.pallas_call(
-        reach_kernel,
-        out_shape=(pltpu.VMEM((rows, width), f32), pltpu.VMEM((1, width), f32)),
+    early = EARLY
+    derivs, rest, sums = pl.pallas_call(
+        functools.partial(reach_kernel, early),
+        out_shape=(pltpu.HBM((rows, width), f32), pltpu.VMEM((rows - early * count, width), f32), pltpu.VMEM((1, width), f32)),
         in_specs=[vmem] * 5,
-        out_specs=(vmem, vmem),
+        out_specs=(hbm, vmem, vmem),
+        scratch_shapes=[pltpu.VMEM((early * count, width), f32), pltpu.SemaphoreType.DMA((early,))],
         compiler_params=params,
         name="reach",
     )(solved, outer, inner, jnp.asarray(reach_weights()), metric.reshape(1, width))
+    derivs = pl.pallas_call(
+        functools.partial(flush_kernel, early),
+        out_shape=pltpu.HBM((rows, width), f32),
+        in_specs=[vmem, hbm],
+        out_specs=hbm,
+        scratch_shapes=[pltpu.SemaphoreType.DMA],
+        input_output_aliases={1: 0},
+        compiler_params=params,
+        name="flush",
+    )(rest, derivs)
     if across & (across - 1) == 0:
         step = 1
         while step < across:

time: 24.8 us -> 21.8 us (0.88)
  local copies, waits for them, and re-layouts: 5.43 us -> 0.01 us
  Pallas kernels: 6.8 us -> 9.27 us
    unnamed x11 -> x6, local copies, waits for them, and re-layouts: 5.43 us -> 0.01 us
    pallas_call x1 -> x2, Pallas kernels: 1.16 us -> 3.39 us  [the longest x1 1.78 us: local(): pl.pallas_call(functools.partial(reach_kernel, early), out_shape=(pltpu.H...]
  transfers between devices with their start and end apart: 4 -> 4, of which waited for: 2 -> 2; matrix products, arithmetic and copies ran while one was open for 9% -> 0% of each run, Pallas kernels for 8% -> 16%
where the time goes in v2:
time: 21.8 us; the launch traced here: 21.7 us
  starting transfers between devices  9.52 us (44%)
  Pallas kernels  9.27 us (43%)
  waiting for transfers between devices  1.66 us (8%)
  between operations  0.69 us (3%)
  other arithmetic  0.52 us (2%)
    ppermute x2, starting transfers between devices, local(): lax.ppermute(sums, 'lines', [(i, i ^ step) for i in range(across)])  6.12 us
    pallas_call x1, Pallas kernels, local(): pl.pallas_call(functools.partial(edges_kernel, groups), out_shape=(pltpu....  4 us
    ppermute x1, starting transfers between devices, local(): outer = lax.ppermute(outer, 'blk', far + [(j, i) for i, j in far])  3.4 us
    pallas_call x1, Pallas kernels, local(): pl.pallas_call(functools.partial(local_kernel, 4), out_shape=pltpu.VMEM((...  1.89 us
    pallas_call x1, Pallas kernels, local(): pl.pallas_call(functools.partial(reach_kernel, early), out_shape=(pltpu.H...  1.78 us
    pallas_call x1, Pallas kernels, local(): pl.pallas_call(functools.partial(flush_kernel, early), out_shape=pltpu.HB...  1.61 us
    ppermute x2, waiting for transfers between devices, local(): lax.ppermute(sums, 'lines', [(i, i ^ step) for i in range(across)])  1.52 us
    div x1, other arithmetic, local(): profile = sums.reshape(width) / (lines * across)  0.52 us
  transfers between devices with their start and end apart: 4, of which 2 were waited for; matrix products, arithmetic and copies ran while one was open for 0% of the time, Pallas kernels for 16%

profile of v2, /device:TPU:0, one launch (start us, length us, event | category | flops | bytes accessed | tf_op | source)
XLA Modules:
  0.0 21.7 jit_solution(4591018365674841830)
XLA Ops:
  0.6 0.0 copy-start
  0.6 4.0 %edges.1 = (bf16[9216,256]{1,0:T(8,128)(2,1)S(1)}, f32[144,128]{1,0:T(8,128)S(1)}, f32[144,128]{1,0:T(8,128)S(1)}) custom-call(f32[9216,128]{1,0:T(8,128)} %bitcast.7, bf16[256,256]{1,0:T(8,128)(2,1)} %constant.9.clone.weights_hbm), custom_call_target="tpu_custom_call" | custom-call | tf_op jit(solution)/shard_map/edges/pallas_call | solution.py:176
  4.6 3.4 %collective-permute-start = (f32[144,128]{1,0:T(8,128)S(1)}, f32[144,128]{1,0:T(8,128)S(1)}, u32[]{:S(2)}, u32[]{:S(2)}) collective-permute-start(f32[144,128]{1,0:T(8,128)S(1)} %get-tuple-element.9), channel_id=1, source_target_pairs={{4,8},{12,16},{20,24},{28,0},{8,4},{16,12},{24,20},{0,28},{5,9},{1... | collective-permute-start | bytes 221192 | tf_op jit(solution)/shard_map/ppermute | solution.py:195
  8.0 0.0 collective-permute-start.1
  8.0 0.0 copy-done
  8.1 0.0 copy-start.1
  8.1 0.0 copy-start.2
  8.1 1.9 %local.1.solved_ref = f32[9216,128]{1,0:T(8,128)S(1)} custom-call(bf16[9216,256]{1,0:T(8,128)(2,1)S(1)} %get-tuple-element.8.split_ref, bf16[256,256]{1,0:T(8,128)(2,1)S(1)} %copy-done), custom_call_target="tpu_custom_call" | custom-call | tf_op jit(solution)/shard_map/local/pallas_call | solution.py:197
  10.0 0.1 collective-permute-done.outer_ref
  10.1 0.0 collective-permute-done.1.inner_ref
  10.1 0.0 copy-done.1
  10.1 0.0 copy-done.2
  10.1 1.8 %reach.1 = (f32[9216,128]{1,0:T(8,128)}, f32[5760,128]{1,0:T(8,128)S(1)}, f32[1,128]{1,0:T(1,128)S(1)}) custom-call(f32[9216,128]{1,0:T(8,128)S(1)} %local.1.solved_ref, f32[144,128]{1,0:T(8,128)S(1)} %collective-permute-done.outer_ref, f32[144,128]{1,0:T(8,128)S(1)} %collective-permute-done.1.inner_ref, bf16[256,256]{1,0:T(8,128)(2,1)S(1)} %copy-done.1, ...), custom_call_target="tpu_custom_call" | custom-call | tf_op jit(solution)/shard_map/reach/pallas_call | solution.py:206
  11.9 3.1 %collective-permute-start.2 = (f32[1,128]{1,0:T(1,128)S(1)}, f32[1,128]{1,0:T(1,128)S(1)}, u32[]{:S(2)}, u32[]{:S(2)}) collective-permute-start(f32[1,128]{1,0:T(1,128)S(1)} %get-tuple-element.13), channel_id=1, source_target_pairs={{0,1},{1,0},{2,3},{3,2},{4,5},{5,4},{6,7},{7,6},{8,9},{9,8},{10,11... | collective-permute-start | bytes 1544 | tf_op jit(solution)/shard_map/ppermute | solution.py:228
  15.0 1.5 %collective-permute-done.2 = f32[1,128]{1,0:T(1,128)S(1)} collective-permute-done((f32[1,128]{1,0:T(1,128)S(1)}, f32[1,128]{1,0:T(1,128)S(1)}, u32[]{:S(2)}, u32[]{:S(2)}) %collective-permute-start.2) | collective-permute-done | bytes 544 | tf_op jit(solution)/shard_map/ppermute | solution.py:228
  16.5 3.0 %collective-permute-start.3 = (f32[1,128]{1,0:T(1,128)S(1)}, f32[1,128]{1,0:T(1,128)S(1)}, u32[]{:S(2)}, u32[]{:S(2)}) collective-permute-start(f32[1,128]{1,0:T(1,128)S(1)} %add.6), channel_id=1, source_target_pairs={{0,2},{1,3},{2,0},{3,1},{4,6},{5,7},{6,4},{7,5},{8,10},{9,11},{10,... | collective-permute-start | bytes 1544 | tf_op jit(solution)/shard_map/ppermute | solution.py:228
  19.5 1.6 %flush.1 = f32[9216,128]{1,0:T(8,128)} custom-call(f32[5760,128]{1,0:T(8,128)S(1)} %get-tuple-element.11.rest_ref, f32[9216,128]{1,0:T(8,128)} %get-tuple-element.12.derivs_ref), custom_call_target="tpu_custom_call", output_to_operand_aliasing={{}: (1, {})} | custom-call | tf_op jit(solution)/shard_map/flush/pallas_call | solution.py:215
  21.1 0.0 collective-permute-done.3
  21.2 0.5 %multiply_bitcast_fusion = f32[128]{0:T(128)} fusion(f32[1,128]{1,0:T(1,128)S(1)} %add.6, f32[1,128]{1,0:T(1,128)S(1)} %collective-permute-done.3), kind=kLoop, calls=%fused_computation | loop fusion | flops 256 | bytes 1536 | tf_op jit(solution)/shard_map/div | solution.py:232
  (1 shorter events, 0.0 us)
Async XLA Ops:
  0.6 7.4 %copy-start = (bf16[256,256]{1,0:T(8,128)(2,1)S(1)}, bf16[256,256]{1,0:T(8,128)(2,1)}, u32[]{:S(2)}) copy-start(bf16[256,256]{1,0:T(8,128)(2,1)} %constant.10.clone.weights_ref) | copy-start | bytes 393220
  4.6 5.4 %collective-permute-start = (f32[144,128]{1,0:T(8,128)S(1)}, f32[144,128]{1,0:T(8,128)S(1)}, u32[]{:S(2)}, u32[]{:S(2)}) collective-permute-start(f32[144,128]{1,0:T(8,128)S(1)} %get-tuple-element.9), channel_id=1, source_target_pairs={{4,8},{12,16},{20,24},{28,0},{8,4},{16,12},{24,20},{0,28},{5,9},{1... | collective-permute-start | bytes 221192 | tf_op jit(solution)/shard_map/ppermute | solution.py:195
  8.0 2.0 %collective-permute-start.1 = (f32[144,128]{1,0:T(8,128)S(1)}, f32[144,128]{1,0:T(8,128)S(1)}, u32[]{:S(2)}, u32[]{:S(2)}) collective-permute-start(f32[144,128]{1,0:T(8,128)S(1)} %get-tuple-element.10), channel_id=1, source_target_pairs={{0,4},{4,0},{8,12},{12,8},{16,20},{20,16},{24,28},{28,24},{1,5},{5... | collective-permute-start | bytes 221192 | tf_op jit(solution)/shard_map/ppermute | solution.py:196
  8.1 2.0 %copy-start.1 = (bf16[256,256]{1,0:T(8,128)(2,1)S(1)}, bf16[256,256]{1,0:T(8,128)(2,1)}, u32[]{:S(2)}) copy-start(bf16[256,256]{1,0:T(8,128)(2,1)} %constant.11.clone.weights_ref) | copy-start | bytes 393220
  8.1 2.0 %copy-start.2 = (f32[128]{0:T(128)S(1)}, f32[128]{0:T(128)}, u32[]{:S(2)}) copy-start(f32[128]{0:T(128)} %param.6) | copy-start | bytes 1540
  11.9 4.6 %collective-permute-start.2 = (f32[1,128]{1,0:T(1,128)S(1)}, f32[1,128]{1,0:T(1,128)S(1)}, u32[]{:S(2)}, u32[]{:S(2)}) collective-permute-start(f32[1,128]{1,0:T(1,128)S(1)} %get-tuple-element.13), channel_id=1, source_target_pairs={{0,1},{1,0},{2,3},{3,2},{4,5},{5,4},{6,7},{7,6},{8,9},{9,8},{10,11... | collective-permute-start | bytes 1544 | tf_op jit(solution)/shard_map/ppermute | solution.py:228
  16.5 4.6 %collective-permute-start.3 = (f32[1,128]{1,0:T(1,128)S(1)}, f32[1,128]{1,0:T(1,128)S(1)}, u32[]{:S(2)}, u32[]{:S(2)}) collective-permute-start(f32[1,128]{1,0:T(1,128)S(1)} %add.6), channel_id=1, source_target_pairs={{0,2},{1,3},{2,0},{3,1},{4,6},{5,7},{6,4},{7,5},{8,10},{9,11},{10,... | collective-permute-start | bytes 1544 | tf_op jit(solution)/shard_map/ppermute | solution.py:228

commit v3 on v1

--- a/solution.py
+++ b/solution.py
@@ -65,14 +65,17 @@
     return lax.rem(lax.axis_index("blk"), 2)
 
 
-def edges_kernel(groups, velocity_ref, weights_ref, split_ref, outer_ref, inner_ref, buffer, packed, sems):
+def edges_kernel(groups, velocity_ref, weights_hbm, split_ref, outer_ref, inner_ref, buffer, packed, weights_ref, sems):
     rows = velocity_ref.shape[0]
     span, count = rows // groups, rows // CHUNKS
+    fetch = pltpu.make_async_copy(weights_hbm, weights_ref, sems.at[groups])
+    fetch.start()
     copies = []
     for g in range(groups):
         part = pl.ds(g * span, span)
         copies.append(pltpu.make_async_copy(velocity_ref.at[part], buffer.at[part], sems.at[g]))
         copies[-1].start()
+    fetch.wait()
     weights = weights_ref[...]
     owner = lax.broadcasted_iota(jnp.int32, (count, WIDTH), 1) % HALF // 2
     per = CHUNKS // groups
@@ -141,6 +144,14 @@
     sums_ref[...] = jnp.sum(sums, axis=0, keepdims=True)
 
 
+def flush_kernel(start, rows, values_ref, *refs):
+    out_ref, sem = refs[-2:]
+    part = pl.ds(start, rows)
+    copy = pltpu.make_async_copy(values_ref.at[part], out_ref.at[part], sem)
+    copy.start()
+    copy.wait()
+
+
 def local(velocity, metric):
     parts, lines, width = velocity.shape
     rows = parts * lines
@@ -148,9 +159,11 @@
     blocks, across = lax.axis_size("blk"), lax.axis_size("lines")
     assert width == WIDTH and rows % (CHUNKS * 32) == 0 and blocks % 2 == 0
     vmem = pl.BlockSpec(memory_space=pltpu.VMEM)
+    hbm = pl.BlockSpec(memory_space=pltpu.HBM)
+    in_hbm = functools.partial(pltpu.with_memory_space_constraint, memory_space=pltpu.HBM)
     params = pltpu.CompilerParams(vmem_limit_bytes=LIMIT)
     f32 = jnp.float32
-    groups = 8
+    groups = 4
     halves, outer, inner = pl.pallas_call(
         functools.partial(edges_kernel, groups),
         out_shape=(
@@ -158,12 +171,17 @@
             pltpu.VMEM((count // 2, width), f32),
             pltpu.VMEM((count // 2, width), f32),
         ),
-        in_specs=[pl.BlockSpec(memory_space=pl.ANY), vmem],
+        in_specs=[hbm, hbm],
         out_specs=(vmem, vmem, vmem),
-        scratch_shapes=[pltpu.VMEM((rows, width), f32), pltpu.VMEM((count, width), f32), pltpu.SemaphoreType.DMA((groups,))],
+        scratch_shapes=[
+            pltpu.VMEM((rows, width), f32),
+            pltpu.VMEM((count, width), f32),
+            pltpu.VMEM((2 * width, 2 * width), jnp.bfloat16),
+            pltpu.SemaphoreType.DMA((groups + 1,)),
+        ],
         compiler_params=params,
         name="edges",
-    )(velocity.reshape(rows, width), jnp.asarray(edge_weights()))
+    )(in_hbm(velocity.reshape(rows, width)), in_hbm(jnp.asarray(edge_weights())))
     far = [(i, (i + 1) % blocks) for i in range(1, blocks, 2)]
     outer = lax.ppermute(outer, "blk", far + [(j, i) for i, j in far])
     inner = lax.ppermute(inner, "blk", [(i, i ^ 1) for i in range(blocks)])
@@ -175,7 +193,7 @@
         compiler_params=params,
         name="local",
     )(halves, jnp.asarray(local_weights()))
-    derivs, sums = pl.pallas_call(
+    values, sums = pl.pallas_call(
         reach_kernel,
         out_shape=(pltpu.VMEM((rows, width), f32), pltpu.VMEM((1, width), f32)),
         in_specs=[vmem] * 5,
@@ -183,13 +201,31 @@
         compiler_params=params,
         name="reach",
     )(solved, outer, inner, jnp.asarray(reach_weights()), metric.reshape(1, width))
+
+    def flush(start, size, *derivs):
+        return pl.pallas_call(
+            functools.partial(flush_kernel, start, size),
+            out_shape=pltpu.HBM((rows, width), f32),
+            in_specs=[vmem] + [hbm] * len(derivs),
+            out_specs=hbm,
+            scratch_shapes=[pltpu.SemaphoreType.DMA],
+            input_output_aliases={1: 0} if derivs else {},
+            compiler_params=params,
+            name="flush",
+        )(values, *derivs)
+
+    derivs = flush(0, rows // 2)
     if across & (across - 1) == 0:
         step = 1
         while step < across:
-            sums = sums + lax.ppermute(sums, "lines", [(i, i ^ step) for i in range(across)])
+            other = lax.ppermute(sums, "lines", [(i, i ^ step) for i in range(across)])
+            if step == 1:
+                other, derivs = lax.optimization_barrier((other, derivs))
+            sums = sums + other
             step *= 2
     else:
         sums = lax.psum(sums, "lines")
+    derivs = flush(rows // 2, rows - rows // 2, derivs)
     profile = sums.reshape(width) / (lines * across)
     return derivs.reshape(velocity.shape), profile
 

time: 24.8 us -> 20.5 us (0.83)
  local copies, waits for them, and re-layouts: 5.43 us -> 0.01 us
  Pallas kernels: 6.8 us -> 9.3 us
  waiting for transfers between devices: 1.67 us -> 0.34 us
    unnamed x11 -> x6, local copies, waits for them, and re-layouts: 5.43 us -> 0.01 us
    pallas_call x0 -> x2, Pallas kernels: none -> 2.82 us  [flush(): pl.pallas_call(functools.partial(flush_kernel, start, size), out_shape=pl...]
    ppermute x2, waiting for transfers between devices: 1.52 us -> 0.2 us  [local(): other = lax.ppermute(sums, 'lines', [(i, i ^ step) for i in range(across)])]
    pallas_call x1, Pallas kernels: 3.77 us -> 3.47 us  [local(): pl.pallas_call(functools.partial(edges_kernel, groups), out_shape=(pltpu....]
  transfers between devices with their start and end apart: 4 -> 4, of which waited for: 2 -> 3; matrix products, arithmetic and copies ran while one was open for 9% -> 0% of each run, Pallas kernels for 8% -> 23%
where the time goes in v3:
time: 20.5 us; the launch traced here: 20.4 us
  starting transfers between devices  9.53 us (46%)
  Pallas kernels  9.3 us (45%)
  between operations  0.69 us (3%)
  other arithmetic  0.52 us (3%)
  waiting for transfers between devices  0.34 us (2%)
    ppermute x2, starting transfers between devices, local(): other = lax.ppermute(sums, 'lines', [(i, i ^ step) for i in range(across)])  6.13 us
    pallas_call x1, Pallas kernels, local(): pl.pallas_call(functools.partial(edges_kernel, groups), out_shape=(pltpu....  3.47 us
    ppermute x1, starting transfers between devices, local(): outer = lax.ppermute(outer, 'blk', far + [(j, i) for i, j in far])  3.4 us
    pallas_call x2, Pallas kernels, flush(): pl.pallas_call(functools.partial(flush_kernel, start, size), out_shape=pl...  2.82 us
    pallas_call x1, Pallas kernels, local(): pl.pallas_call(functools.partial(local_kernel, 4), out_shape=pltpu.VMEM((...  1.87 us
    pallas_call x1, Pallas kernels, local(): pl.pallas_call(reach_kernel, out_shape=(pltpu.VMEM((rows, width), f32), p...  1.13 us
    div x1, other arithmetic, local(): profile = sums.reshape(width) / (lines * across)  0.51 us
  transfers between devices with their start and end apart: 4, of which 3 were waited for; matrix products, arithmetic and copies ran while one was open for 0% of the time, Pallas kernels for 23%

profile of v3, /device:TPU:0, one launch (start us, length us, event | category | flops | bytes accessed | tf_op | source)
XLA Modules:
  0.0 20.4 jit_solution(3013590028290185690)
XLA Ops:
  0.6 0.0 copy-start
  0.6 3.5 %edges.1 = (bf16[9216,256]{1,0:T(8,128)(2,1)S(1)}, f32[144,128]{1,0:T(8,128)S(1)}, f32[144,128]{1,0:T(8,128)S(1)}) custom-call(f32[9216,128]{1,0:T(8,128)} %bitcast.7, bf16[256,256]{1,0:T(8,128)(2,1)} %constant.9.clone.weights_hbm), custom_call_target="tpu_custom_call" | custom-call | tf_op jit(solution)/shard_map/edges/pallas_call | solution.py:167
  4.1 3.4 %collective-permute-start = (f32[144,128]{1,0:T(8,128)S(1)}, f32[144,128]{1,0:T(8,128)S(1)}, u32[]{:S(2)}, u32[]{:S(2)}) collective-permute-start(f32[144,128]{1,0:T(8,128)S(1)} %get-tuple-element.10), channel_id=1, source_target_pairs={{4,8},{12,16},{20,24},{28,0},{8,4},{16,12},{24,20},{0,28},{5,9},{1... | collective-permute-start | bytes 221192 | tf_op jit(solution)/shard_map/ppermute | solution.py:186
  7.5 0.0 collective-permute-start.1
  7.5 0.0 copy-done
  7.5 0.0 copy-start.1
  7.5 0.0 copy-start.2
  7.5 1.9 %local.1.solved_ref = f32[9216,128]{1,0:T(8,128)S(1)} custom-call(bf16[9216,256]{1,0:T(8,128)(2,1)S(1)} %get-tuple-element.9.split_ref, bf16[256,256]{1,0:T(8,128)(2,1)S(1)} %copy-done), custom_call_target="tpu_custom_call" | custom-call | tf_op jit(solution)/shard_map/local/pallas_call | solution.py:188
  9.4 0.1 collective-permute-done.outer_ref
  9.6 0.0 collective-permute-done.1.inner_ref
  9.6 0.0 copy-done.1
  9.6 0.0 copy-done.2
  9.6 1.1 %reach.1 = (f32[9216,128]{1,0:T(8,128)S(1)}, f32[1,128]{1,0:T(1,128)S(1)}) custom-call(f32[9216,128]{1,0:T(8,128)S(1)} %local.1.solved_ref, f32[144,128]{1,0:T(8,128)S(1)} %collective-permute-done.outer_ref, f32[144,128]{1,0:T(8,128)S(1)} %collective-permute-done.1.inner_ref, bf16[256,256]{1,0:T(8,128)(2,1)S(1)} %copy-done.1, f32[1,128]{1,0:T(1,128)S(1)} %bitcast.5), custom_call_target="tpu_custom_call" | custom-call | tf_op jit(solution)/shard_map/reach/pallas_call | solution.py:196
  10.7 3.1 %collective-permute-start.2 = (f32[1,128]{1,0:T(1,128)S(1)}, f32[1,128]{1,0:T(1,128)S(1)}, u32[]{:S(2)}, u32[]{:S(2)}) collective-permute-start(f32[1,128]{1,0:T(1,128)S(1)} %get-tuple-element.13), channel_id=1, source_target_pairs={{0,1},{1,0},{2,3},{3,2},{4,5},{5,4},{6,7},{7,6},{8,9},{9,8},{10,11... | collective-permute-start | bytes 1544 | tf_op jit(solution)/shard_map/ppermute | solution.py:221
  13.8 1.4 %flush.2.refs_0_ = f32[9216,128]{1,0:T(8,128)} custom-call(f32[9216,128]{1,0:T(8,128)S(1)} %get-tuple-element.12.values_ref), custom_call_target="tpu_custom_call" | custom-call | tf_op jit(solution)/shard_map/flush/pallas_call | solution.py:206
  15.2 0.1 collective-permute-done.2
  15.3 3.0 %collective-permute-start.3 = (f32[1,128]{1,0:T(1,128)S(1)}, f32[1,128]{1,0:T(1,128)S(1)}, u32[]{:S(2)}, u32[]{:S(2)}) collective-permute-start(f32[1,128]{1,0:T(1,128)S(1)} %add.6), channel_id=1, source_target_pairs={{0,2},{1,3},{2,0},{3,1},{4,6},{5,7},{6,4},{7,5},{8,10},{9,11},{10,... | collective-permute-start | bytes 1544 | tf_op jit(solution)/shard_map/ppermute | solution.py:221
  18.4 1.4 %flush.3 = f32[9216,128]{1,0:T(8,128)} custom-call(f32[9216,128]{1,0:T(8,128)S(1)} %get-tuple-element.12.values_ref, f32[9216,128]{1,0:T(8,128)} %flush.2.refs_0_), custom_call_target="tpu_custom_call", output_to_operand_aliasing={{}: (1, {})} | custom-call | tf_op jit(solution)/shard_map/flush/pallas_call | solution.py:206
  19.8 0.1 collective-permute-done.3
  19.9 0.5 %multiply_bitcast_fusion = f32[128]{0:T(128)} fusion(f32[1,128]{1,0:T(1,128)S(1)} %add.6, f32[1,128]{1,0:T(1,128)S(1)} %collective-permute-done.3), kind=kLoop, calls=%fused_computation | loop fusion | flops 256 | bytes 1536 | tf_op jit(solution)/shard_map/div | solution.py:229
  (1 shorter events, 0.0 us)
Async XLA Ops:
  0.6 6.9 %copy-start = (bf16[256,256]{1,0:T(8,128)(2,1)S(1)}, bf16[256,256]{1,0:T(8,128)(2,1)}, u32[]{:S(2)}) copy-start(bf16[256,256]{1,0:T(8,128)(2,1)} %constant.10.clone.weights_ref) | copy-start | bytes 393220
  4.1 5.4 %collective-permute-start = (f32[144,128]{1,0:T(8,128)S(1)}, f32[144,128]{1,0:T(8,128)S(1)}, u32[]{:S(2)}, u32[]{:S(2)}) collective-permute-start(f32[144,128]{1,0:T(8,128)S(1)} %get-tuple-element.10), channel_id=1, source_target_pairs={{4,8},{12,16},{20,24},{28,0},{8,4},{16,12},{24,20},{0,28},{5,9},{1... | collective-permute-start | bytes 221192 | tf_op jit(solution)/shard_map/ppermute | solution.py:186
  7.5 2.0 %collective-permute-start.1 = (f32[144,128]{1,0:T(8,128)S(1)}, f32[144,128]{1,0:T(8,128)S(1)}, u32[]{:S(2)}, u32[]{:S(2)}) collective-permute-start(f32[144,128]{1,0:T(8,128)S(1)} %get-tuple-element.11), channel_id=1, source_target_pairs={{0,4},{4,0},{8,12},{12,8},{16,20},{20,16},{24,28},{28,24},{1,5},{5... | collective-permute-start | bytes 221192 | tf_op jit(solution)/shard_map/ppermute | solution.py:187
  7.5 2.0 %copy-start.1 = (bf16[256,256]{1,0:T(8,128)(2,1)S(1)}, bf16[256,256]{1,0:T(8,128)(2,1)}, u32[]{:S(2)}) copy-start(bf16[256,256]{1,0:T(8,128)(2,1)} %constant.11.clone.weights_ref) | copy-start | bytes 393220
  7.5 2.0 %copy-start.2 = (f32[128]{0:T(128)S(1)}, f32[128]{0:T(128)}, u32[]{:S(2)}) copy-start(f32[128]{0:T(128)} %param.6) | copy-start | bytes 1540
  10.7 4.6 %collective-permute-start.2 = (f32[1,128]{1,0:T(1,128)S(1)}, f32[1,128]{1,0:T(1,128)S(1)}, u32[]{:S(2)}, u32[]{:S(2)}) collective-permute-start(f32[1,128]{1,0:T(1,128)S(1)} %get-tuple-element.13), channel_id=1, source_target_pairs={{0,1},{1,0},{2,3},{3,2},{4,5},{5,4},{6,7},{7,6},{8,9},{9,8},{10,11... | collective-permute-start | bytes 1544 | tf_op jit(solution)/shard_map/ppermute | solution.py:221
  15.3 4.5 %collective-permute-start.3 = (f32[1,128]{1,0:T(1,128)S(1)}, f32[1,128]{1,0:T(1,128)S(1)}, u32[]{:S(2)}, u32[]{:S(2)}) collective-permute-start(f32[1,128]{1,0:T(1,128)S(1)} %add.6), channel_id=1, source_target_pairs={{0,2},{1,3},{2,0},{3,1},{4,6},{5,7},{6,4},{7,5},{8,10},{9,11},{10,... | collective-permute-start | bytes 1544 | tf_op jit(solution)/shard_map/ppermute | solution.py:221

commit v4 on v3

--- a/solution.py
+++ b/solution.py
@@ -37,8 +37,7 @@
 def local_weights():
     lag = np.arange(WIDTH)[None, :] - np.arange(WIDTH)[:, None]
     weights = np.sign(lag) * (GAIN * powers(np.abs(lag)) - NEAR * (np.abs(lag) == 1))
-    both = np.concatenate(split(weights), axis=1)
-    return np.concatenate([both, both], axis=0)
+    return np.concatenate(split(weights), axis=1)
 
 
 def edge_weights():
@@ -47,47 +46,42 @@
     weights = np.zeros((WIDTH, WIDTH))
     for lane in range(WIDTH):
         weights[:, lane] = columns[2 * (lane // HALF) + lane % 2]
-    both = np.concatenate(split(weights), axis=1)
-    return np.concatenate([both, both], axis=0)
-
-
-def reach_weights():
+    return np.concatenate(split(weights), axis=1)
+
+
+def reach_rows():
     station = np.arange(WIDTH)
     rows = [GAIN * powers(station + 1), -NEAR * (station == 0), -GAIN * powers(WIDTH - station), NEAR * (station == WIDTH - 1)]
-    weights = np.zeros((WIDTH, 2 * WIDTH))
-    for lane in range(WIDTH):
-        start = WIDTH * (lane % 4 // 2)
-        weights[lane, start : start + WIDTH] = rows[2 * (lane // HALF) + lane % 2]
-    return np.concatenate(split(weights), axis=0)
+    return np.stack(rows).astype(np.float32)
 
 
 def parity():
     return lax.rem(lax.axis_index("blk"), 2)
 
 
-def edges_kernel(groups, velocity_ref, weights_hbm, split_ref, outer_ref, inner_ref, buffer, packed, weights_ref, sems):
-    rows = velocity_ref.shape[0]
-    span, count = rows // groups, rows // CHUNKS
-    fetch = pltpu.make_async_copy(weights_hbm, weights_ref, sems.at[groups])
+def halves(value):
+    high = value.astype(jnp.bfloat16)
+    return high, (value - high.astype(jnp.float32)).astype(jnp.bfloat16)
+
+
+def edges_kernel(sizes, velocity_hbm, weights_hbm, velocity_ref, outer_ref, inner_ref, packed, weights_ref, sems):
+    count = velocity_ref.shape[0] // CHUNKS
+    fetch = pltpu.make_async_copy(weights_hbm, weights_ref, sems.at[len(sizes)])
+    copies, firsts = [], np.cumsum([0] + sizes)
+    for g, size in enumerate(sizes):
+        part = pl.ds(int(firsts[g]) * count, size * count)
+        copies.append(pltpu.make_async_copy(velocity_hbm.at[part], velocity_ref.at[part], sems.at[g]))
+    copies[0].start()
     fetch.start()
-    copies = []
-    for g in range(groups):
-        part = pl.ds(g * span, span)
-        copies.append(pltpu.make_async_copy(velocity_ref.at[part], buffer.at[part], sems.at[g]))
-        copies[-1].start()
+    for copy in copies[1:]:
+        copy.start()
     fetch.wait()
-    weights = weights_ref[...]
+    weights = jnp.concatenate([weights_ref[...]] * 2, axis=0)
     owner = lax.broadcasted_iota(jnp.int32, (count, WIDTH), 1) % HALF // 2
-    per = CHUNKS // groups
-    for g in range(groups):
-        copies[g].wait()
-        for c in range(g * per, (g + 1) * per):
-            part = pl.ds(c * count, count)
-            value = buffer[part, :]
-            high = value.astype(jnp.bfloat16)
-            low = (value - high.astype(jnp.float32)).astype(jnp.bfloat16)
-            both = jnp.concatenate([high, low], axis=1)
-            split_ref[part, :] = both
+    for g, copy in enumerate(copies):
+        copy.wait()
+        for c in range(int(firsts[g]), int(firsts[g + 1])):
+            both = jnp.concatenate(halves(velocity_ref[pl.ds(c * count, count), :]), axis=1)
             out = jnp.dot(both, weights, preferred_element_type=jnp.float32)
             pltpu.store(packed, out[:, :WIDTH] + out[:, WIDTH:], mask=owner == c)
     lower = packed[: count // 2, :]
@@ -100,20 +94,30 @@
     inner_ref[...] = jnp.where(even, last, first)
 
 
-def local_kernel(steps, split_ref, weights_ref, out_ref):
-    count = split_ref.shape[0] // steps
-    weights = weights_ref[...]
-
-    def step(s, carry):
-        part = pl.ds(pl.multiple_of(s * count, count), count)
-        out = jnp.dot(split_ref[part, :], weights, preferred_element_type=jnp.float32)
-        out_ref[part, :] = out[:, :WIDTH] + out[:, WIDTH:]
-        return carry
-
-    lax.fori_loop(0, steps, step, 0)
-
-
-def reach_kernel(solved_ref, outer_ref, inner_ref, weights_ref, metric_ref, out_ref, sums_ref):
+def local_kernel(velocity_ref, weights_ref, rows_ref, metric_ref, out_ref, scaled_ref):
+    count = velocity_ref.shape[0] // CHUNKS
+    weights = jnp.concatenate([weights_ref[...]] * 2, axis=0)
+    metric = jnp.broadcast_to(metric_ref[...], (count, WIDTH))
+    for c in range(CHUNKS):
+        part = pl.ds(c * count, count)
+        both = jnp.concatenate(halves(velocity_ref[part, :]), axis=1)
+        out = jnp.dot(both, weights, preferred_element_type=jnp.float32)
+        out_ref[part, :] = (out[:, :WIDTH] + out[:, WIDTH:]) * metric
+    scaled = rows_ref[...] * metric_ref[...]
+    lane = lax.broadcasted_iota(jnp.int32, (WIDTH, WIDTH), 0)
+    spread = jnp.zeros((WIDTH, WIDTH), jnp.float32)
+    for side in range(2):
+        for q in range(2):
+            row = 2 * side + q
+            spread = jnp.where((lane // HALF == side) & (lane % 2 == q), scaled[row : row + 1, :], spread)
+    zero = jnp.zeros_like(spread)
+    first = lane % 4 // 2 == 0
+    high, low = halves(jnp.concatenate([jnp.where(first, spread, zero), jnp.where(first, zero, spread)], axis=1))
+    scaled_ref[:WIDTH, :] = high
+    scaled_ref[WIDTH:, :] = low
+
+
+def reach_kernel(solved_ref, outer_ref, inner_ref, weights_ref, out_ref, sums_ref):
     count = solved_ref.shape[0] // CHUNKS
     even = parity() == 0
     left = jnp.where(even, outer_ref[...], inner_ref[...])
@@ -130,7 +134,6 @@
     slot = slot.astype(jnp.bfloat16)
     zero = jnp.zeros_like(high)
     weights = weights_ref[...]
-    metric = jnp.broadcast_to(metric_ref[...], (count, WIDTH))
     sums = jnp.zeros((8, WIDTH), jnp.float32)
     for p in range(CHUNKS // 2):
         mine = jnp.where(slot == p, high, zero)
@@ -138,7 +141,7 @@
         out = jnp.dot(rows, weights, preferred_element_type=jnp.float32)
         for e in range(2):
             part = pl.ds((2 * p + e) * count, count)
-            value = (solved_ref[part, :] + out[:, e * WIDTH : (e + 1) * WIDTH]) * metric
+            value = solved_ref[part, :] + out[:, e * WIDTH : (e + 1) * WIDTH]
             out_ref[part, :] = value
             sums = sums + jnp.sum((value * value).reshape(count // 8, 8, WIDTH), axis=0)
     sums_ref[...] = jnp.sum(sums, axis=0, keepdims=True)
@@ -163,21 +166,20 @@
     in_hbm = functools.partial(pltpu.with_memory_space_constraint, memory_space=pltpu.HBM)
     params = pltpu.CompilerParams(vmem_limit_bytes=LIMIT)
     f32 = jnp.float32
-    groups = 4
-    halves, outer, inner = pl.pallas_call(
-        functools.partial(edges_kernel, groups),
+    sizes = [4, 8, 10, 10]
+    stations, outer, inner = pl.pallas_call(
+        functools.partial(edges_kernel, sizes),
         out_shape=(
-            pltpu.VMEM((rows, 2 * width), jnp.bfloat16),
+            pltpu.VMEM((rows, width), f32),
             pltpu.VMEM((count // 2, width), f32),
             pltpu.VMEM((count // 2, width), f32),
         ),
         in_specs=[hbm, hbm],
         out_specs=(vmem, vmem, vmem),
         scratch_shapes=[
-            pltpu.VMEM((rows, width), f32),
             pltpu.VMEM((count, width), f32),
-            pltpu.VMEM((2 * width, 2 * width), jnp.bfloat16),
-            pltpu.SemaphoreType.DMA((groups + 1,)),
+            pltpu.VMEM((width, 2 * width), jnp.bfloat16),
+            pltpu.SemaphoreType.DMA((len(sizes) + 1,)),
         ],
         compiler_params=params,
         name="edges",
@@ -185,22 +187,22 @@
     far = [(i, (i + 1) % blocks) for i in range(1, blocks, 2)]
     outer = lax.ppermute(outer, "blk", far + [(j, i) for i, j in far])
     inner = lax.ppermute(inner, "blk", [(i, i ^ 1) for i in range(blocks)])
-    solved = pl.pallas_call(
-        functools.partial(local_kernel, 4),
-        out_shape=pltpu.VMEM((rows, width), f32),
-        in_specs=[vmem, vmem],
-        out_specs=vmem,
+    solved, scaled = pl.pallas_call(
+        local_kernel,
+        out_shape=(pltpu.VMEM((rows, width), f32), pltpu.VMEM((2 * width, 2 * width), jnp.bfloat16)),
+        in_specs=[vmem] * 4,
+        out_specs=(vmem, vmem),
         compiler_params=params,
         name="local",
-    )(halves, jnp.asarray(local_weights()))
+    )(stations, jnp.asarray(local_weights()), jnp.asarray(reach_rows()), metric.reshape(1, width))
     values, sums = pl.pallas_call(
         reach_kernel,
         out_shape=(pltpu.VMEM((rows, width), f32), pltpu.VMEM((1, width), f32)),
-        in_specs=[vmem] * 5,
+        in_specs=[vmem] * 4,
         out_specs=(vmem, vmem),
         compiler_params=params,
         name="reach",
-    )(solved, outer, inner, jnp.asarray(reach_weights()), metric.reshape(1, width))
+    )(solved, outer, inner, scaled)
 
     def flush(start, size, *derivs):
         return pl.pallas_call(

time: 20.5 us -> 20.2 us (0.985)
  Pallas kernels: 9.3 us -> 8.51 us
  waiting for transfers between devices: 0.34 us -> 0.78 us
    pallas_call x2, Pallas kernels: 5.34 us -> 4.69 us  [the longest x1 3.27 us: local(): pl.pallas_call(functools.partial(edges_kernel, sizes), out_shape=(pltpu.V...]
    ppermute x1, waiting for transfers between devices: 0.14 us -> 0.58 us  [local(): outer = lax.ppermute(outer, 'blk', far + [(j, i) for i, j in far])]
  transfers between devices with their start and end apart: 4 -> 4, of which waited for: 3 -> 3; matrix products, arithmetic and copies ran while one was open for 0% -> 0% of each run, Pallas kernels for 23% -> 21%
where the time goes in v4:
time: 20.2 us; the launch traced here: 20 us
  starting transfers between devices  9.48 us (47%)
  Pallas kernels  8.51 us (42%)
  waiting for transfers between devices  0.78 us (4%)
  between operations  0.7 us (3%)
  other arithmetic  0.52 us (3%)
    ppermute x2, starting transfers between devices, local(): other = lax.ppermute(sums, 'lines', [(i, i ^ step) for i in range(across)])  6.07 us
    ppermute x1, starting transfers between devices, local(): outer = lax.ppermute(outer, 'blk', far + [(j, i) for i, j in far])  3.41 us
    pallas_call x1, Pallas kernels, local(): pl.pallas_call(functools.partial(edges_kernel, sizes), out_shape=(pltpu.V...  3.27 us
    pallas_call x2, Pallas kernels, flush(): pl.pallas_call(functools.partial(flush_kernel, start, size), out_shape=pl...  2.82 us
    pallas_call x1, Pallas kernels, local(): pl.pallas_call(local_kernel, out_shape=(pltpu.VMEM((rows, width), f32), p...  1.43 us
    pallas_call x1, Pallas kernels, local(): pl.pallas_call(reach_kernel, out_shape=(pltpu.VMEM((rows, width), f32), p...  0.99 us
    ppermute x1, waiting for transfers between devices, local(): outer = lax.ppermute(outer, 'blk', far + [(j, i) for i, j in far])  0.58 us
    div x1, other arithmetic, local(): profile = sums.reshape(width) / (lines * across)  0.51 us
  transfers between devices with their start and end apart: 4, of which 3 were waited for; matrix products, arithmetic and copies ran while one was open for 0% of the time, Pallas kernels for 21%

profile of v4, /device:TPU:0, one launch (start us, length us, event | category | flops | bytes accessed | tf_op | source)
XLA Modules:
  0.0 20.0 jit_solution(16972179210247540122)
XLA Ops:
  0.6 0.0 copy-start
  0.6 0.0 copy-start.1
  0.7 0.0 copy-start.2
  0.7 3.3 %edges.1 = (f32[9216,128]{1,0:T(8,128)S(1)}, f32[144,128]{1,0:T(8,128)S(1)}, f32[144,128]{1,0:T(8,128)S(1)}) custom-call(f32[9216,128]{1,0:T(8,128)} %bitcast.7, bf16[128,256]{1,0:T(8,128)(2,1)} %constant.9.clone.weights_hbm), custom_call_target="tpu_custom_call" | custom-call | tf_op jit(solution)/shard_map/edges/pallas_call | solution.py:170
  3.9 3.4 %collective-permute-start = (f32[144,128]{1,0:T(8,128)S(1)}, f32[144,128]{1,0:T(8,128)S(1)}, u32[]{:S(2)}, u32[]{:S(2)}) collective-permute-start(f32[144,128]{1,0:T(8,128)S(1)} %get-tuple-element.13), channel_id=1, source_target_pairs={{4,8},{12,16},{20,24},{28,0},{8,4},{16,12},{24,20},{0,28},{5,9},{1... | collective-permute-start | bytes 221192 | tf_op jit(solution)/shard_map/ppermute | solution.py:188
  7.3 0.0 collective-permute-start.1
  7.4 0.0 copy-done
  7.4 0.0 copy-done.1
  7.4 0.0 copy-done.2
  7.4 1.4 %local.1 = (f32[9216,128]{1,0:T(8,128)S(1)}, bf16[256,256]{1,0:T(8,128)(2,1)S(1)}) custom-call(f32[9216,128]{1,0:T(8,128)S(1)} %get-tuple-element.11.velocity_ref, bf16[128,256]{1,0:T(8,128)(2,1)S(1)} %copy-done, f32[4,128]{1,0:T(4,128)S(1)} %copy-done.1, f32[1,128]{1,0:T(1,128)S(1)} %bitcast.5), custom_call_target="tpu_custom_call" | custom-call | tf_op jit(solution)/shard_map/local/pallas_call | solution.py:190
  8.8 0.6 %collective-permute-done.outer_ref = f32[144,128]{1,0:T(8,128)S(1)} collective-permute-done((f32[144,128]{1,0:T(8,128)S(1)}, f32[144,128]{1,0:T(8,128)S(1)}, u32[]{:S(2)}, u32[]{:S(2)}) %collective-permute-start) | collective-permute-done | bytes 73760 | tf_op jit(solution)/shard_map/ppermute | solution.py:188
  9.4 0.0 collective-permute-done.1.inner_ref
  9.4 1.0 %reach.1 = (f32[9216,128]{1,0:T(8,128)S(1)}, f32[1,128]{1,0:T(1,128)S(1)}) custom-call(f32[9216,128]{1,0:T(8,128)S(1)} %get-tuple-element.12.solved_ref, f32[144,128]{1,0:T(8,128)S(1)} %collective-permute-done.outer_ref, f32[144,128]{1,0:T(8,128)S(1)} %collective-permute-done.1.inner_ref, bf16[256,256]{1,0:T(8,128)(2,1)S(1)} %get-tuple-element.15.weights_ref), custom_call_target="tpu_custom_call" | custom-call | tf_op jit(solution)/shard_map/reach/pallas_call | solution.py:198
  10.4 3.1 %collective-permute-start.2 = (f32[1,128]{1,0:T(1,128)S(1)}, f32[1,128]{1,0:T(1,128)S(1)}, u32[]{:S(2)}, u32[]{:S(2)}) collective-permute-start(f32[1,128]{1,0:T(1,128)S(1)} %get-tuple-element.17), channel_id=1, source_target_pairs={{0,1},{1,0},{2,3},{3,2},{4,5},{5,4},{6,7},{7,6},{8,9},{9,8},{10,11... | collective-permute-start | bytes 1544 | tf_op jit(solution)/shard_map/ppermute | solution.py:223
  13.5 1.4 %flush.2.refs_0_ = f32[9216,128]{1,0:T(8,128)} custom-call(f32[9216,128]{1,0:T(8,128)S(1)} %get-tuple-element.16.values_ref), custom_call_target="tpu_custom_call" | custom-call | tf_op jit(solution)/shard_map/flush/pallas_call | solution.py:208
  14.9 0.1 collective-permute-done.2
  15.0 3.0 %collective-permute-start.3 = (f32[1,128]{1,0:T(1,128)S(1)}, f32[1,128]{1,0:T(1,128)S(1)}, u32[]{:S(2)}, u32[]{:S(2)}) collective-permute-start(f32[1,128]{1,0:T(1,128)S(1)} %add.6), channel_id=1, source_target_pairs={{0,2},{1,3},{2,0},{3,1},{4,6},{5,7},{6,4},{7,5},{8,10},{9,11},{10,... | collective-permute-start | bytes 1544 | tf_op jit(solution)/shard_map/ppermute | solution.py:223
  18.0 1.4 %flush.3 = f32[9216,128]{1,0:T(8,128)} custom-call(f32[9216,128]{1,0:T(8,128)S(1)} %get-tuple-element.16.values_ref, f32[9216,128]{1,0:T(8,128)} %flush.2.refs_0_), custom_call_target="tpu_custom_call", output_to_operand_aliasing={{}: (1, {})} | custom-call | tf_op jit(solution)/shard_map/flush/pallas_call | solution.py:208
  19.4 0.1 collective-permute-done.3
  19.5 0.5 %multiply_bitcast_fusion = f32[128]{0:T(128)} fusion(f32[1,128]{1,0:T(1,128)S(1)} %add.6, f32[1,128]{1,0:T(1,128)S(1)} %collective-permute-done.3), kind=kLoop, calls=%fused_computation | loop fusion | flops 256 | bytes 1536 | tf_op jit(solution)/shard_map/div | solution.py:231
  (1 shorter events, 0.0 us)
Async XLA Ops:
  0.6 6.7 %copy-start = (bf16[128,256]{1,0:T(8,128)(2,1)S(1)}, bf16[128,256]{1,0:T(8,128)(2,1)}, u32[]{:S(2)}) copy-start(bf16[128,256]{1,0:T(8,128)(2,1)} %constant.10.clone.weights_ref) | copy-start | bytes 196612
  0.6 6.7 %copy-start.1 = (f32[4,128]{1,0:T(4,128)S(1)}, f32[4,128]{1,0:T(4,128)}, u32[]{:S(2)}) copy-start(f32[4,128]{1,0:T(4,128)} %constant.11.clone.rows_ref) | copy-start | bytes 6148
  0.7 6.7 %copy-start.2 = (f32[128]{0:T(128)S(1)}, f32[128]{0:T(128)}, u32[]{:S(2)}) copy-start(f32[128]{0:T(128)} %param.6) | copy-start | bytes 1540
  3.9 5.4 %collective-permute-start = (f32[144,128]{1,0:T(8,128)S(1)}, f32[144,128]{1,0:T(8,128)S(1)}, u32[]{:S(2)}, u32[]{:S(2)}) collective-permute-start(f32[144,128]{1,0:T(8,128)S(1)} %get-tuple-element.13), channel_id=1, source_target_pairs={{4,8},{12,16},{20,24},{28,0},{8,4},{16,12},{24,20},{0,28},{5,9},{1... | collective-permute-start | bytes 221192 | tf_op jit(solution)/shard_map/ppermute | solution.py:188
  7.3 2.0 %collective-permute-start.1 = (f32[144,128]{1,0:T(8,128)S(1)}, f32[144,128]{1,0:T(8,128)S(1)}, u32[]{:S(2)}, u32[]{:S(2)}) collective-permute-start(f32[144,128]{1,0:T(8,128)S(1)} %get-tuple-element.14), channel_id=1, source_target_pairs={{0,4},{4,0},{8,12},{12,8},{16,20},{20,16},{24,28},{28,24},{1,5},{5... | collective-permute-start | bytes 221192 | tf_op jit(solution)/shard_map/ppermute | solution.py:189
  10.4 4.6 %collective-permute-start.2 = (f32[1,128]{1,0:T(1,128)S(1)}, f32[1,128]{1,0:T(1,128)S(1)}, u32[]{:S(2)}, u32[]{:S(2)}) collective-permute-start(f32[1,128]{1,0:T(1,128)S(1)} %get-tuple-element.17), channel_id=1, source_target_pairs={{0,1},{1,0},{2,3},{3,2},{4,5},{5,4},{6,7},{7,6},{8,9},{9,8},{10,11... | collective-permute-start | bytes 1544 | tf_op jit(solution)/shard_map/ppermute | solution.py:223
  15.0 4.5 %collective-permute-start.3 = (f32[1,128]{1,0:T(1,128)S(1)}, f32[1,128]{1,0:T(1,128)S(1)}, u32[]{:S(2)}, u32[]{:S(2)}) collective-permute-start(f32[1,128]{1,0:T(1,128)S(1)} %add.6), channel_id=1, source_target_pairs={{0,2},{1,3},{2,0},{3,1},{4,6},{5,7},{6,4},{7,5},{8,10},{9,11},{10,... | collective-permute-start | bytes 1544 | tf_op jit(solution)/shard_map/ppermute | solution.py:223

commit v5 on v4

--- a/solution.py
+++ b/solution.py
@@ -21,6 +21,7 @@
 WIDTH = 128
 HALF = WIDTH // 2
 CHUNKS = 32
+EDGE = 16
 LIMIT = 24 * 2**20
 
 
@@ -40,13 +41,27 @@
     return np.concatenate(split(weights), axis=1)
 
 
-def edge_weights():
+def edge_columns():
     station = np.arange(WIDTH)
     columns = [powers(station), station == 0, powers(WIDTH - 1 - station), station == WIDTH - 1]
     weights = np.zeros((WIDTH, WIDTH))
     for lane in range(WIDTH):
         weights[:, lane] = columns[2 * (lane // HALF) + lane % 2]
-    return np.concatenate(split(weights), axis=1)
+    return weights
+
+
+def edge_weights():
+    return np.concatenate(split(edge_columns()), axis=1)
+
+
+def low_weights():
+    weights = np.zeros((WIDTH, WIDTH))
+    columns = edge_columns()
+    for station in list(range(EDGE)) + list(range(WIDTH - EDGE, WIDTH)):
+        for lane in range(WIDTH):
+            chunk = lane % HALF // 2
+            weights[(station + 2 * EDGE * (chunk % 4)) % WIDTH, lane] = columns[station, lane]
+    return split(weights)[0]
 
 
 def reach_rows():
@@ -64,29 +79,51 @@
     return high, (value - high.astype(jnp.float32)).astype(jnp.bfloat16)
 
 
-def edges_kernel(sizes, velocity_hbm, weights_hbm, velocity_ref, outer_ref, inner_ref, packed, weights_ref, sems):
+def edges_kernel(sizes, velocity_hbm, weights_hbm, lows_hbm, velocity_ref, outer_ref, inner_ref, packed, small, weights_ref, lows_ref, sems):
     count = velocity_ref.shape[0] // CHUNKS
     fetch = pltpu.make_async_copy(weights_hbm, weights_ref, sems.at[len(sizes)])
+    fetch_lows = pltpu.make_async_copy(lows_hbm, lows_ref, sems.at[len(sizes) + 1])
     copies, firsts = [], np.cumsum([0] + sizes)
     for g, size in enumerate(sizes):
         part = pl.ds(int(firsts[g]) * count, size * count)
         copies.append(pltpu.make_async_copy(velocity_hbm.at[part], velocity_ref.at[part], sems.at[g]))
     copies[0].start()
     fetch.start()
+    fetch_lows.start()
     for copy in copies[1:]:
         copy.start()
     fetch.wait()
-    weights = jnp.concatenate([weights_ref[...]] * 2, axis=0)
-    owner = lax.broadcasted_iota(jnp.int32, (count, WIDTH), 1) % HALF // 2
+    fetch_lows.wait()
+    weights = weights_ref[...]
+    odd = lax.broadcasted_iota(jnp.int32, weights.shape, 1) % 4 // 2
+    zero = jnp.zeros_like(weights)
+    odd = odd.astype(jnp.bfloat16)
+    weights = jnp.concatenate([jnp.where(odd == 0, weights, zero), jnp.where(odd == 0, zero, weights)], axis=0)
+    lows = lows_ref[...]
+    lane = lax.broadcasted_iota(jnp.int32, (count, WIDTH), 1)
+    owner = lane % HALF // 2
     for g, copy in enumerate(copies):
         copy.wait()
-        for c in range(int(firsts[g]), int(firsts[g + 1])):
-            both = jnp.concatenate(halves(velocity_ref[pl.ds(c * count, count), :]), axis=1)
-            out = jnp.dot(both, weights, preferred_element_type=jnp.float32)
-            pltpu.store(packed, out[:, :WIDTH] + out[:, WIDTH:], mask=owner == c)
-    lower = packed[: count // 2, :]
-    upper = packed[count // 2 :, :]
-    lane = lax.broadcasted_iota(jnp.int32, lower.shape, 1)
+        for first in range(int(firsts[g]), int(firsts[g + 1]), 4):
+            for pair in range(2):
+                highs = []
+                for e in range(2):
+                    turn = 2 * pair + e
+                    value = velocity_ref[pl.ds((first + turn) * count, count), :]
+                    highs.append(value.astype(jnp.bfloat16))
+                    low = value - highs[-1].astype(jnp.float32)
+                    if turn == 0:
+                        merged = low
+                    else:
+                        inside = (lane + WIDTH + EDGE - 2 * EDGE * turn) % WIDTH < 2 * EDGE
+                        merged = jnp.where(inside, pltpu.roll(low, 2 * EDGE * turn, 1), merged)
+                out = jnp.dot(jnp.concatenate(highs, axis=1), weights, preferred_element_type=jnp.float32)
+                pltpu.store(packed, out[:, :WIDTH] + out[:, WIDTH:], mask=owner // 2 == first // 2 + pair)
+            out = jnp.dot(merged.astype(jnp.bfloat16), lows, preferred_element_type=jnp.float32)
+            pltpu.store(small, out, mask=owner // 4 == first // 4)
+    lower = packed[: count // 2, :] + small[: count // 2, :]
+    upper = packed[count // 2 :, :] + small[count // 2 :, :]
+    lane = lane[: count // 2]
     first = jnp.where(lane < HALF, lower, pltpu.roll(upper, HALF, 1))
     last = jnp.where(lane < HALF, pltpu.roll(lower, HALF, 1), upper)
     even = parity() == 0
@@ -166,7 +203,7 @@
     in_hbm = functools.partial(pltpu.with_memory_space_constraint, memory_space=pltpu.HBM)
     params = pltpu.CompilerParams(vmem_limit_bytes=LIMIT)
     f32 = jnp.float32
-    sizes = [4, 8, 10, 10]
+    sizes = [8, 8, 8, 8]
     stations, outer, inner = pl.pallas_call(
         functools.partial(edges_kernel, sizes),
         out_shape=(
@@ -174,16 +211,18 @@
             pltpu.VMEM((count // 2, width), f32),
             pltpu.VMEM((count // 2, width), f32),
         ),
-        in_specs=[hbm, hbm],
+        in_specs=[hbm] * 3,
         out_specs=(vmem, vmem, vmem),
         scratch_shapes=[
             pltpu.VMEM((count, width), f32),
+            pltpu.VMEM((count, width), f32),
             pltpu.VMEM((width, 2 * width), jnp.bfloat16),
-            pltpu.SemaphoreType.DMA((len(sizes) + 1,)),
+            pltpu.VMEM((width, width), jnp.bfloat16),
+            pltpu.SemaphoreType.DMA((len(sizes) + 2,)),
         ],
         compiler_params=params,
         name="edges",
-    )(in_hbm(velocity.reshape(rows, width)), in_hbm(jnp.asarray(edge_weights())))
+    )(in_hbm(velocity.reshape(rows, width)), in_hbm(jnp.asarray(edge_weights())), in_hbm(jnp.asarray(low_weights())))
     far = [(i, (i + 1) % blocks) for i in range(1, blocks, 2)]
     outer = lax.ppermute(outer, "blk", far + [(j, i) for i, j in far])
     inner = lax.ppermute(inner, "blk", [(i, i ^ 1) for i in range(blocks)])

time: 20.2 us -> 19.9 us (0.985)
  Pallas kernels: 8.51 us -> 8.16 us
    pallas_call x1, Pallas kernels: 3.27 us -> 2.93 us  [local(): pl.pallas_call(functools.partial(edges_kernel, sizes), out_shape=(pltpu.V...]
  transfers between devices with their start and end apart: 4 -> 4, of which waited for: 3 -> 3; matrix products, arithmetic and copies ran while one was open for 0% -> 0% of each run, Pallas kernels for 21% -> 22%
where the time goes in v5:
time: 19.9 us; the launch traced here: 19.7 us
  starting transfers between devices  9.52 us (48%)
  Pallas kernels  8.16 us (41%)
  waiting for transfers between devices  0.79 us (4%)
  between operations  0.7 us (4%)
  other arithmetic  0.52 us (3%)
    ppermute x2, starting transfers between devices, local(): other = lax.ppermute(sums, 'lines', [(i, i ^ step) for i in range(across)])  6.12 us
    ppermute x1, starting transfers between devices, local(): outer = lax.ppermute(outer, 'blk', far + [(j, i) for i, j in far])  3.4 us
    pallas_call x1, Pallas kernels, local(): pl.pallas_call(functools.partial(edges_kernel, sizes), out_shape=(pltpu.V...  2.93 us
    pallas_call x2, Pallas kernels, flush(): pl.pallas_call(functools.partial(flush_kernel, start, size), out_shape=pl...  2.82 us
    pallas_call x1, Pallas kernels, local(): pl.pallas_call(local_kernel, out_shape=(pltpu.VMEM((rows, width), f32), p...  1.41 us
    pallas_call x1, Pallas kernels, local(): pl.pallas_call(reach_kernel, out_shape=(pltpu.VMEM((rows, width), f32), p...  0.99 us
    ppermute x1, waiting for transfers between devices, local(): outer = lax.ppermute(outer, 'blk', far + [(j, i) for i, j in far])  0.59 us
    div x1, other arithmetic, local(): profile = sums.reshape(width) / (lines * across)  0.51 us
  transfers between devices with their start and end apart: 4, of which 3 were waited for; matrix products, arithmetic and copies ran while one was open for 0% of the time, Pallas kernels for 22%

profile of v5, /device:TPU:0, one launch (start us, length us, event | category | flops | bytes accessed | tf_op | source)
XLA Modules:
  0.0 19.7 jit_solution(16154977578664847727)
XLA Ops:
  0.6 0.0 copy-start
  0.6 0.0 copy-start.1
  0.7 0.0 copy-start.2
  0.7 2.9 %edges.1 = (f32[9216,128]{1,0:T(8,128)S(1)}, f32[144,128]{1,0:T(8,128)S(1)}, f32[144,128]{1,0:T(8,128)S(1)}) custom-call(f32[9216,128]{1,0:T(8,128)} %bitcast.7, bf16[128,256]{1,0:T(8,128)(2,1)} %constant.11.clone.weights_hbm, bf16[128,128]{1,0:T(8,128)(2,1)} %constant.12.clone.lows_hbm), custom_call_target="tpu_custom_call" | custom-call | tf_op jit(solution)/shard_map/edges/pallas_call | solution.py:207
  3.6 3.4 %collective-permute-start = (f32[144,128]{1,0:T(8,128)S(1)}, f32[144,128]{1,0:T(8,128)S(1)}, u32[]{:S(2)}, u32[]{:S(2)}) collective-permute-start(f32[144,128]{1,0:T(8,128)S(1)} %get-tuple-element.13), channel_id=1, source_target_pairs={{4,8},{12,16},{20,24},{28,0},{8,4},{16,12},{24,20},{0,28},{5,9},{1... | collective-permute-start | bytes 221192 | tf_op jit(solution)/shard_map/ppermute | solution.py:227
  7.0 0.0 collective-permute-start.1
  7.0 0.0 copy-done
  7.0 0.0 copy-done.1
  7.0 0.0 copy-done.2
  7.0 1.4 %local.1 = (f32[9216,128]{1,0:T(8,128)S(1)}, bf16[256,256]{1,0:T(8,128)(2,1)S(1)}) custom-call(f32[9216,128]{1,0:T(8,128)S(1)} %get-tuple-element.11.velocity_ref, bf16[128,256]{1,0:T(8,128)(2,1)S(1)} %copy-done, f32[4,128]{1,0:T(4,128)S(1)} %copy-done.1, f32[1,128]{1,0:T(1,128)S(1)} %bitcast.5), custom_call_target="tpu_custom_call" | custom-call | tf_op jit(solution)/shard_map/local/pallas_call | solution.py:229
  8.4 0.6 %collective-permute-done.outer_ref = f32[144,128]{1,0:T(8,128)S(1)} collective-permute-done((f32[144,128]{1,0:T(8,128)S(1)}, f32[144,128]{1,0:T(8,128)S(1)}, u32[]{:S(2)}, u32[]{:S(2)}) %collective-permute-start) | collective-permute-done | bytes 73760 | tf_op jit(solution)/shard_map/ppermute | solution.py:227
  9.0 0.0 collective-permute-done.1.inner_ref
  9.0 1.0 %reach.1 = (f32[9216,128]{1,0:T(8,128)S(1)}, f32[1,128]{1,0:T(1,128)S(1)}) custom-call(f32[9216,128]{1,0:T(8,128)S(1)} %get-tuple-element.12.solved_ref, f32[144,128]{1,0:T(8,128)S(1)} %collective-permute-done.outer_ref, f32[144,128]{1,0:T(8,128)S(1)} %collective-permute-done.1.inner_ref, bf16[256,256]{1,0:T(8,128)(2,1)S(1)} %get-tuple-element.15.weights_ref), custom_call_target="tpu_custom_call" | custom-call | tf_op jit(solution)/shard_map/reach/pallas_call | solution.py:237
  10.0 3.1 %collective-permute-start.2 = (f32[1,128]{1,0:T(1,128)S(1)}, f32[1,128]{1,0:T(1,128)S(1)}, u32[]{:S(2)}, u32[]{:S(2)}) collective-permute-start(f32[1,128]{1,0:T(1,128)S(1)} %get-tuple-element.17), channel_id=1, source_target_pairs={{0,1},{1,0},{2,3},{3,2},{4,5},{5,4},{6,7},{7,6},{8,9},{9,8},{10,11... | collective-permute-start | bytes 1544 | tf_op jit(solution)/shard_map/ppermute | solution.py:262
  13.1 1.4 %flush.2.refs_0_ = f32[9216,128]{1,0:T(8,128)} custom-call(f32[9216,128]{1,0:T(8,128)S(1)} %get-tuple-element.16.values_ref), custom_call_target="tpu_custom_call" | custom-call | tf_op jit(solution)/shard_map/flush/pallas_call | solution.py:247
  14.5 0.1 collective-permute-done.2
  14.6 3.0 %collective-permute-start.3 = (f32[1,128]{1,0:T(1,128)S(1)}, f32[1,128]{1,0:T(1,128)S(1)}, u32[]{:S(2)}, u32[]{:S(2)}) collective-permute-start(f32[1,128]{1,0:T(1,128)S(1)} %add.6), channel_id=1, source_target_pairs={{0,2},{1,3},{2,0},{3,1},{4,6},{5,7},{6,4},{7,5},{8,10},{9,11},{10,... | collective-permute-start | bytes 1544 | tf_op jit(solution)/shard_map/ppermute | solution.py:262
  17.7 1.4 %flush.3 = f32[9216,128]{1,0:T(8,128)} custom-call(f32[9216,128]{1,0:T(8,128)S(1)} %get-tuple-element.16.values_ref, f32[9216,128]{1,0:T(8,128)} %flush.2.refs_0_), custom_call_target="tpu_custom_call", output_to_operand_aliasing={{}: (1, {})} | custom-call | tf_op jit(solution)/shard_map/flush/pallas_call | solution.py:247
  19.1 0.1 collective-permute-done.3
  19.2 0.5 %multiply_bitcast_fusion = f32[128]{0:T(128)} fusion(f32[1,128]{1,0:T(1,128)S(1)} %add.6, f32[1,128]{1,0:T(1,128)S(1)} %collective-permute-done.3), kind=kLoop, calls=%fused_computation | loop fusion | flops 256 | bytes 1536 | tf_op jit(solution)/shard_map/div | solution.py:270
  (1 shorter events, 0.0 us)
Async XLA Ops:
  0.6 6.4 %copy-start = (bf16[128,256]{1,0:T(8,128)(2,1)S(1)}, bf16[128,256]{1,0:T(8,128)(2,1)}, u32[]{:S(2)}) copy-start(bf16[128,256]{1,0:T(8,128)(2,1)} %constant.13.clone.weights_ref) | copy-start | bytes 196612
  0.6 6.4 %copy-start.1 = (f32[4,128]{1,0:T(4,128)S(1)}, f32[4,128]{1,0:T(4,128)}, u32[]{:S(2)}) copy-start(f32[4,128]{1,0:T(4,128)} %constant.14.clone.rows_ref) | copy-start | bytes 6148
  0.7 6.4 %copy-start.2 = (f32[128]{0:T(128)S(1)}, f32[128]{0:T(128)}, u32[]{:S(2)}) copy-start(f32[128]{0:T(128)} %param.7) | copy-start | bytes 1540
  3.6 5.4 %collective-permute-start = (f32[144,128]{1,0:T(8,128)S(1)}, f32[144,128]{1,0:T(8,128)S(1)}, u32[]{:S(2)}, u32[]{:S(2)}) collective-permute-start(f32[144,128]{1,0:T(8,128)S(1)} %get-tuple-element.13), channel_id=1, source_target_pairs={{4,8},{12,16},{20,24},{28,0},{8,4},{16,12},{24,20},{0,28},{5,9},{1... | collective-permute-start | bytes 221192 | tf_op jit(solution)/shard_map/ppermute | solution.py:227
  7.0 2.0 %collective-permute-start.1 = (f32[144,128]{1,0:T(8,128)S(1)}, f32[144,128]{1,0:T(8,128)S(1)}, u32[]{:S(2)}, u32[]{:S(2)}) collective-permute-start(f32[144,128]{1,0:T(8,128)S(1)} %get-tuple-element.14), channel_id=1, source_target_pairs={{0,4},{4,0},{8,12},{12,8},{16,20},{20,16},{24,28},{28,24},{1,5},{5... | collective-permute-start | bytes 221192 | tf_op jit(solution)/shard_map/ppermute | solution.py:228
  10.0 4.6 %collective-permute-start.2 = (f32[1,128]{1,0:T(1,128)S(1)}, f32[1,128]{1,0:T(1,128)S(1)}, u32[]{:S(2)}, u32[]{:S(2)}) collective-permute-start(f32[1,128]{1,0:T(1,128)S(1)} %get-tuple-element.17), channel_id=1, source_target_pairs={{0,1},{1,0},{2,3},{3,2},{4,5},{5,4},{6,7},{7,6},{8,9},{9,8},{10,11... | collective-permute-start | bytes 1544 | tf_op jit(solution)/shard_map/ppermute | solution.py:262
  14.6 4.6 %collective-permute-start.3 = (f32[1,128]{1,0:T(1,128)S(1)}, f32[1,128]{1,0:T(1,128)S(1)}, u32[]{:S(2)}, u32[]{:S(2)}) collective-permute-start(f32[1,128]{1,0:T(1,128)S(1)} %add.6), channel_id=1, source_target_pairs={{0,2},{1,3},{2,0},{3,1},{4,6},{5,7},{6,4},{7,5},{8,10},{9,11},{10,... | collective-permute-start | bytes 1544 | tf_op jit(solution)/shard_map/ppermute | solution.py:262

commit v6 on v5

--- a/solution.py
+++ b/solution.py
@@ -131,54 +131,60 @@
     inner_ref[...] = jnp.where(even, last, first)
 
 
-def local_kernel(velocity_ref, weights_ref, rows_ref, metric_ref, out_ref, scaled_ref):
+def reach_weights(rows, side):
+    lane = lax.broadcasted_iota(jnp.int32, (WIDTH, WIDTH), 0)
+    pick = [jnp.where(side == 0, rows[q : q + 1, :], rows[q + 2 : q + 3, :]) for q in range(2)]
+    spread = jnp.where(lane % 2 == 0, pick[0], pick[1])
+    high = spread.astype(jnp.bfloat16).astype(jnp.float32)
+    spread = jnp.where(lane // 4 % 2 == 0, high, spread - high)
+    zero = jnp.zeros_like(spread)
+    first = lane % 4 // 2 == 0
+    both = jnp.concatenate([jnp.where(first, spread, zero), jnp.where(first, zero, spread)], axis=1)
+    return both.astype(jnp.bfloat16)
+
+
+def reach(values, weights):
+    slot = lax.broadcasted_iota(jnp.int32, values.shape, 1) // 4
+    high = values.astype(jnp.bfloat16).astype(jnp.float32)
+    low = values - high
+    even = slot % 2 == 0
+    highs = [jnp.where(even, high, pltpu.roll(high, 4, 1)), jnp.where(even, pltpu.roll(high, WIDTH - 4, 1), high)]
+    lows = [pltpu.roll(low, 8, 1), pltpu.roll(low, 4, 1)]
+    highs = [x.astype(jnp.bfloat16) for x in highs]
+    lows = [x.astype(jnp.bfloat16) for x in lows]
+    pair = (slot // 2).astype(jnp.bfloat16)
+    slot = slot.astype(jnp.bfloat16)
+    zero = jnp.zeros_like(lows[0])
+    slots = WIDTH // 4
+    for k in range(slots // 2):
+        rows = []
+        for s in (k, k + slots // 2):
+            mine = jnp.where(slot == (2 * (s // 2) + 2) % slots, lows[k % 2], zero)
+            rows.append(jnp.where(pair == s // 2, highs[k % 2], mine))
+        yield k, jnp.dot(jnp.concatenate(rows, axis=0), weights, preferred_element_type=jnp.float32)
+
+
+def near_kernel(velocity_ref, inner_ref, weights_ref, rows_ref, metric_ref, out_ref, far_ref):
     count = velocity_ref.shape[0] // CHUNKS
     weights = jnp.concatenate([weights_ref[...]] * 2, axis=0)
     metric = jnp.broadcast_to(metric_ref[...], (count, WIDTH))
-    for c in range(CHUNKS):
-        part = pl.ds(c * count, count)
-        both = jnp.concatenate(halves(velocity_ref[part, :]), axis=1)
-        out = jnp.dot(both, weights, preferred_element_type=jnp.float32)
-        out_ref[part, :] = (out[:, :WIDTH] + out[:, WIDTH:]) * metric
     scaled = rows_ref[...] * metric_ref[...]
-    lane = lax.broadcasted_iota(jnp.int32, (WIDTH, WIDTH), 0)
-    spread = jnp.zeros((WIDTH, WIDTH), jnp.float32)
-    for side in range(2):
-        for q in range(2):
-            row = 2 * side + q
-            spread = jnp.where((lane // HALF == side) & (lane % 2 == q), scaled[row : row + 1, :], spread)
-    zero = jnp.zeros_like(spread)
-    first = lane % 4 // 2 == 0
-    high, low = halves(jnp.concatenate([jnp.where(first, spread, zero), jnp.where(first, zero, spread)], axis=1))
-    scaled_ref[:WIDTH, :] = high
-    scaled_ref[WIDTH:, :] = low
-
-
-def reach_kernel(solved_ref, outer_ref, inner_ref, weights_ref, out_ref, sums_ref):
+    far_ref[...] = reach_weights(scaled, parity())
+    for k, added in reach(inner_ref[...], reach_weights(scaled, 1 - parity())):
+        for e in range(2):
+            part = pl.ds((2 * k + e) * count, count)
+            both = jnp.concatenate(halves(velocity_ref[part, :]), axis=1)
+            out = jnp.dot(both, weights, preferred_element_type=jnp.float32)
+            out_ref[part, :] = (out[:, :WIDTH] + out[:, WIDTH:]) * metric + added[:, e * WIDTH : (e + 1) * WIDTH]
+
+
+def far_kernel(solved_ref, outer_ref, weights_ref, out_ref, sums_ref):
     count = solved_ref.shape[0] // CHUNKS
-    even = parity() == 0
-    left = jnp.where(even, outer_ref[...], inner_ref[...])
-    right = jnp.where(even, inner_ref[...], outer_ref[...])
-    lane = lax.broadcasted_iota(jnp.int32, left.shape, 1)
-    lower = jnp.where(lane < HALF, left, pltpu.roll(right, HALF, 1))
-    upper = jnp.where(lane < HALF, pltpu.roll(left, HALF, 1), right)
-    packed = jnp.concatenate([lower, upper], axis=0)
-    slot = lax.broadcasted_iota(jnp.int32, packed.shape, 1) % HALF // 4
-    high = packed.astype(jnp.bfloat16).astype(jnp.float32)
-    low = packed - high
-    low = jnp.where(slot % 2 == 0, pltpu.roll(low, WIDTH - 4, 1), pltpu.roll(low, 4, 1))
-    high, low = high.astype(jnp.bfloat16), low.astype(jnp.bfloat16)
-    slot = slot.astype(jnp.bfloat16)
-    zero = jnp.zeros_like(high)
-    weights = weights_ref[...]
     sums = jnp.zeros((8, WIDTH), jnp.float32)
-    for p in range(CHUNKS // 2):
-        mine = jnp.where(slot == p, high, zero)
-        rows = jnp.concatenate([jnp.where(slot == (p ^ 1), low, mine), mine], axis=1)
-        out = jnp.dot(rows, weights, preferred_element_type=jnp.float32)
+    for k, added in reach(outer_ref[...], weights_ref[...]):
         for e in range(2):
-            part = pl.ds((2 * p + e) * count, count)
-            value = solved_ref[part, :] + out[:, e * WIDTH : (e + 1) * WIDTH]
+            part = pl.ds((2 * k + e) * count, count)
+            value = solved_ref[part, :] + added[:, e * WIDTH : (e + 1) * WIDTH]
             out_ref[part, :] = value
             sums = sums + jnp.sum((value * value).reshape(count // 8, 8, WIDTH), axis=0)
     sums_ref[...] = jnp.sum(sums, axis=0, keepdims=True)
@@ -226,22 +232,22 @@
     far = [(i, (i + 1) % blocks) for i in range(1, blocks, 2)]
     outer = lax.ppermute(outer, "blk", far + [(j, i) for i, j in far])
     inner = lax.ppermute(inner, "blk", [(i, i ^ 1) for i in range(blocks)])
-    solved, scaled = pl.pallas_call(
-        local_kernel,
-        out_shape=(pltpu.VMEM((rows, width), f32), pltpu.VMEM((2 * width, 2 * width), jnp.bfloat16)),
-        in_specs=[vmem] * 4,
+    solved, weights = pl.pallas_call(
+        near_kernel,
+        out_shape=(pltpu.VMEM((rows, width), f32), pltpu.VMEM((width, 2 * width), jnp.bfloat16)),
+        in_specs=[vmem] * 5,
         out_specs=(vmem, vmem),
         compiler_params=params,
-        name="local",
-    )(stations, jnp.asarray(local_weights()), jnp.asarray(reach_rows()), metric.reshape(1, width))
+        name="near",
+    )(stations, inner, jnp.asarray(local_weights()), jnp.asarray(reach_rows()), metric.reshape(1, width))
     values, sums = pl.pallas_call(
-        reach_kernel,
+        far_kernel,
         out_shape=(pltpu.VMEM((rows, width), f32), pltpu.VMEM((1, width), f32)),
-        in_specs=[vmem] * 4,
+        in_specs=[vmem] * 3,
         out_specs=(vmem, vmem),
         compiler_params=params,
-        name="reach",
-    )(solved, outer, inner, scaled)
+        name="far",
+    )(solved, outer, weights)
 
     def flush(start, size, *derivs):
         return pl.pallas_call(

time: 19.9 us -> 19.4 us (0.975)
  starting transfers between devices: 9.52 us -> 8.74 us
  Pallas kernels: 8.16 us -> 8.71 us
  waiting for transfers between devices: 0.79 us -> 0.55 us
    ppermute x2, starting transfers between devices: 6.12 us -> 4.66 us  [local(): other = lax.ppermute(sums, 'lines', [(i, i ^ step) for i in range(across)])]
    ppermute x1, waiting for transfers between devices: 0.59 us -> 0.01 us  [local(): outer = lax.ppermute(outer, 'blk', far + [(j, i) for i, j in far])]
    pallas_call x2, Pallas kernels: 2.4 us -> 2.96 us  [the longest x1 2.12 us: local(): pl.pallas_call(near_kernel, out_shape=(pltpu.VMEM((rows, width), f32), pl...]
    ppermute x1, starting transfers between devices: 0.01 us -> 0.53 us  [local(): inner = lax.ppermute(inner, 'blk', [(i, i ^ 1) for i in range(blocks)])]
    ppermute x2, waiting for transfers between devices: 0.2 us -> 0.54 us  [local(): other = lax.ppermute(sums, 'lines', [(i, i ^ step) for i in range(across)])]
  transfers between devices with their start and end apart: 4 -> 4, of which waited for: 3 -> 2; matrix products, arithmetic and copies ran while one was open for 0% -> 0% of each run, Pallas kernels for 22% -> 26%
where the time goes in v6:
time: 19.4 us; the launch traced here: 19.2 us
  starting transfers between devices  8.74 us (45%)
  Pallas kernels  8.71 us (45%)
  between operations  0.71 us (4%)
  waiting for transfers between devices  0.55 us (3%)
  other arithmetic  0.52 us (3%)
    ppermute x2, starting transfers between devices, local(): other = lax.ppermute(sums, 'lines', [(i, i ^ step) for i in range(across)])  4.66 us
    ppermute x1, starting transfers between devices, local(): outer = lax.ppermute(outer, 'blk', far + [(j, i) for i, j in far])  3.55 us
    pallas_call x1, Pallas kernels, local(): pl.pallas_call(functools.partial(edges_kernel, sizes), out_shape=(pltpu.V...  2.93 us
    pallas_call x2, Pallas kernels, flush(): pl.pallas_call(functools.partial(flush_kernel, start, size), out_shape=pl...  2.82 us
    pallas_call x1, Pallas kernels, local(): pl.pallas_call(near_kernel, out_shape=(pltpu.VMEM((rows, width), f32), pl...  2.12 us
    pallas_call x1, Pallas kernels, local(): pl.pallas_call(far_kernel, out_shape=(pltpu.VMEM((rows, width), f32), plt...  0.85 us
    ppermute x2, waiting for transfers between devices, local(): other = lax.ppermute(sums, 'lines', [(i, i ^ step) for i in range(across)])  0.54 us
    ppermute x1, starting transfers between devices, local(): inner = lax.ppermute(inner, 'blk', [(i, i ^ 1) for i in range(blocks)])  0.53 us
  transfers between devices with their start and end apart: 4, of which 2 were waited for; matrix products, arithmetic and copies ran while one was open for 0% of the time, Pallas kernels for 26%

profile of v6, /device:TPU:0, one launch (start us, length us, event | category | flops | bytes accessed | tf_op | source)
XLA Modules:
  0.0 19.2 jit_solution(18205925093200387829)
XLA Ops:
  0.6 0.0 copy-start
  0.6 0.0 copy-start.1
  0.7 0.0 copy-start.2
  0.7 2.9 %edges.1 = (f32[9216,128]{1,0:T(8,128)S(1)}, f32[144,128]{1,0:T(8,128)S(1)}, f32[144,128]{1,0:T(8,128)S(1)}) custom-call(f32[9216,128]{1,0:T(8,128)} %bitcast.7, bf16[128,256]{1,0:T(8,128)(2,1)} %constant.11.clone.weights_hbm, bf16[128,128]{1,0:T(8,128)(2,1)} %constant.12.clone.lows_hbm), custom_call_target="tpu_custom_call" | custom-call | tf_op jit(solution)/shard_map/edges/pallas_call | solution.py:213
  3.6 0.5 %collective-permute-start = (f32[144,128]{1,0:T(8,128)S(1)}, f32[144,128]{1,0:T(8,128)S(1)}, u32[]{:S(2)}, u32[]{:S(2)}) collective-permute-start(f32[144,128]{1,0:T(8,128)S(1)} %get-tuple-element.12), channel_id=1, source_target_pairs={{0,4},{4,0},{8,12},{12,8},{16,20},{20,16},{24,28},{28,24},{1,5},{5... | collective-permute-start | bytes 221192 | tf_op jit(solution)/shard_map/ppermute | solution.py:234
  4.1 3.5 %collective-permute-start.1 = (f32[144,128]{1,0:T(8,128)S(1)}, f32[144,128]{1,0:T(8,128)S(1)}, u32[]{:S(2)}, u32[]{:S(2)}) collective-permute-start(f32[144,128]{1,0:T(8,128)S(1)} %get-tuple-element.14), channel_id=1, source_target_pairs={{4,8},{12,16},{20,24},{28,0},{8,4},{16,12},{24,20},{0,28},{5,9},{1... | collective-permute-start | bytes 221192 | tf_op jit(solution)/shard_map/ppermute | solution.py:233
  7.7 0.0 collective-permute-done.inner_ref
  7.7 0.0 copy-done
  7.7 0.0 copy-done.1
  7.7 0.0 copy-done.2
  7.7 2.1 %near.1 = (f32[9216,128]{1,0:T(8,128)S(1)}, bf16[128,256]{1,0:T(8,128)(2,1)S(1)}) custom-call(f32[9216,128]{1,0:T(8,128)S(1)} %get-tuple-element.11.velocity_ref, f32[144,128]{1,0:T(8,128)S(1)} %collective-permute-done.inner_ref, bf16[128,256]{1,0:T(8,128)(2,1)S(1)} %copy-done, f32[4,128]{1,0:T(4,128)S(1)} %copy-done.1, f32[1,128]{1,0:T(1,128)S(1)} %bitcast.5), custom_call_target="tpu_custom_call" | custom-call | tf_op jit(solution)/shard_map/near/pallas_call | solution.py:235
  9.8 0.0 collective-permute-done.1.outer_ref
  9.8 0.8 %far.1 = (f32[9216,128]{1,0:T(8,128)S(1)}, f32[1,128]{1,0:T(1,128)S(1)}) custom-call(f32[9216,128]{1,0:T(8,128)S(1)} %get-tuple-element.13.solved_ref, f32[144,128]{1,0:T(8,128)S(1)} %collective-permute-done.1.outer_ref, bf16[128,256]{1,0:T(8,128)(2,1)S(1)} %get-tuple-element.15.weights_ref), custom_call_target="tpu_custom_call" | custom-call | tf_op jit(solution)/shard_map/far/pallas_call | solution.py:243
  10.7 1.9 %collective-permute-start.2 = (f32[1,128]{1,0:T(1,128)S(1)}, f32[1,128]{1,0:T(1,128)S(1)}, u32[]{:S(2)}, u32[]{:S(2)}) collective-permute-start(f32[1,128]{1,0:T(1,128)S(1)} %get-tuple-element.17), channel_id=1, source_target_pairs={{0,1},{1,0},{2,3},{3,2},{4,5},{5,4},{6,7},{7,6},{8,9},{9,8},{10,11... | collective-permute-start | bytes 1544 | tf_op jit(solution)/shard_map/ppermute | solution.py:268
  12.5 1.4 %flush.2.refs_0_ = f32[9216,128]{1,0:T(8,128)} custom-call(f32[9216,128]{1,0:T(8,128)S(1)} %get-tuple-element.16.values_ref), custom_call_target="tpu_custom_call" | custom-call | tf_op jit(solution)/shard_map/flush/pallas_call | solution.py:253
  13.9 0.3 %collective-permute-done.2 = f32[1,128]{1,0:T(1,128)S(1)} collective-permute-done((f32[1,128]{1,0:T(1,128)S(1)}, f32[1,128]{1,0:T(1,128)S(1)}, u32[]{:S(2)}, u32[]{:S(2)}) %collective-permute-start.2) | collective-permute-done | bytes 544 | tf_op jit(solution)/shard_map/ppermute | solution.py:268
  14.3 2.8 %collective-permute-start.3 = (f32[1,128]{1,0:T(1,128)S(1)}, f32[1,128]{1,0:T(1,128)S(1)}, u32[]{:S(2)}, u32[]{:S(2)}) collective-permute-start(f32[1,128]{1,0:T(1,128)S(1)} %add.6), channel_id=1, source_target_pairs={{0,2},{1,3},{2,0},{3,1},{4,6},{5,7},{6,4},{7,5},{8,10},{9,11},{10,... | collective-permute-start | bytes 1544 | tf_op jit(solution)/shard_map/ppermute | solution.py:268
  17.1 1.4 %flush.3 = f32[9216,128]{1,0:T(8,128)} custom-call(f32[9216,128]{1,0:T(8,128)S(1)} %get-tuple-element.16.values_ref, f32[9216,128]{1,0:T(8,128)} %flush.2.refs_0_), custom_call_target="tpu_custom_call", output_to_operand_aliasing={{}: (1, {})} | custom-call | tf_op jit(solution)/shard_map/flush/pallas_call | solution.py:253
  18.5 0.2 %collective-permute-done.3 = f32[1,128]{1,0:T(1,128)S(1)} collective-permute-done((f32[1,128]{1,0:T(1,128)S(1)}, f32[1,128]{1,0:T(1,128)S(1)}, u32[]{:S(2)}, u32[]{:S(2)}) %collective-permute-start.3) | collective-permute-done | bytes 544 | tf_op jit(solution)/shard_map/ppermute | solution.py:268
  18.7 0.5 %multiply_bitcast_fusion = f32[128]{0:T(128)} fusion(f32[1,128]{1,0:T(1,128)S(1)} %add.6, f32[1,128]{1,0:T(1,128)S(1)} %collective-permute-done.3), kind=kLoop, calls=%fused_computation | loop fusion | flops 256 | bytes 1536 | tf_op jit(solution)/shard_map/div | solution.py:276
  (1 shorter events, 0.0 us)
Async XLA Ops:
  0.6 7.0 %copy-start = (bf16[128,256]{1,0:T(8,128)(2,1)S(1)}, bf16[128,256]{1,0:T(8,128)(2,1)}, u32[]{:S(2)}) copy-start(bf16[128,256]{1,0:T(8,128)(2,1)} %constant.13.clone.weights_ref) | copy-start | bytes 196612
  0.6 7.0 %copy-start.1 = (f32[4,128]{1,0:T(4,128)S(1)}, f32[4,128]{1,0:T(4,128)}, u32[]{:S(2)}) copy-start(f32[4,128]{1,0:T(4,128)} %constant.14.clone.rows_ref) | copy-start | bytes 6148
  0.7 7.0 %copy-start.2 = (f32[128]{0:T(128)S(1)}, f32[128]{0:T(128)}, u32[]{:S(2)}) copy-start(f32[128]{0:T(128)} %param.7) | copy-start | bytes 1540
  3.6 4.1 %collective-permute-start = (f32[144,128]{1,0:T(8,128)S(1)}, f32[144,128]{1,0:T(8,128)S(1)}, u32[]{:S(2)}, u32[]{:S(2)}) collective-permute-start(f32[144,128]{1,0:T(8,128)S(1)} %get-tuple-element.12), channel_id=1, source_target_pairs={{0,4},{4,0},{8,12},{12,8},{16,20},{20,16},{24,28},{28,24},{1,5},{5... | collective-permute-start | bytes 221192 | tf_op jit(solution)/shard_map/ppermute | solution.py:234
  4.1 5.7 %collective-permute-start.1 = (f32[144,128]{1,0:T(8,128)S(1)}, f32[144,128]{1,0:T(8,128)S(1)}, u32[]{:S(2)}, u32[]{:S(2)}) collective-permute-start(f32[144,128]{1,0:T(8,128)S(1)} %get-tuple-element.14), channel_id=1, source_target_pairs={{4,8},{12,16},{20,24},{28,0},{8,4},{16,12},{24,20},{0,28},{5,9},{1... | collective-permute-start | bytes 221192 | tf_op jit(solution)/shard_map/ppermute | solution.py:233
  10.7 3.6 %collective-permute-start.2 = (f32[1,128]{1,0:T(1,128)S(1)}, f32[1,128]{1,0:T(1,128)S(1)}, u32[]{:S(2)}, u32[]{:S(2)}) collective-permute-start(f32[1,128]{1,0:T(1,128)S(1)} %get-tuple-element.17), channel_id=1, source_target_pairs={{0,1},{1,0},{2,3},{3,2},{4,5},{5,4},{6,7},{7,6},{8,9},{9,8},{10,11... | collective-permute-start | bytes 1544 | tf_op jit(solution)/shard_map/ppermute | solution.py:268
  14.3 4.4 %collective-permute-start.3 = (f32[1,128]{1,0:T(1,128)S(1)}, f32[1,128]{1,0:T(1,128)S(1)}, u32[]{:S(2)}, u32[]{:S(2)}) collective-permute-start(f32[1,128]{1,0:T(1,128)S(1)} %add.6), channel_id=1, source_target_pairs={{0,2},{1,3},{2,0},{3,1},{4,6},{5,7},{6,4},{7,5},{8,10},{9,11},{10,... | collective-permute-start | bytes 1544 | tf_op jit(solution)/shard_map/ppermute | solution.py:268

commit v7 on v6

--- a/solution.py
+++ b/solution.py
@@ -102,14 +102,18 @@
     lows = lows_ref[...]
     lane = lax.broadcasted_iota(jnp.int32, (count, WIDTH), 1)
     owner = lane % HALF // 2
-    for g, copy in enumerate(copies):
-        copy.wait()
-        for first in range(int(firsts[g]), int(firsts[g + 1]), 4):
+    size = sizes[0]
+
+    def group(g, carry):
+        start = pl.multiple_of(g * (size * count), size * count)
+        part = pl.ds(start, size * count)
+        pltpu.make_async_copy(velocity_hbm.at[part], velocity_ref.at[part], sems.at[g]).wait()
+        for first in range(0, size, 4):
             for pair in range(2):
                 highs = []
                 for e in range(2):
                     turn = 2 * pair + e
-                    value = velocity_ref[pl.ds((first + turn) * count, count), :]
+                    value = velocity_ref[pl.ds(start + (first + turn) * count, count), :]
                     highs.append(value.astype(jnp.bfloat16))
                     low = value - highs[-1].astype(jnp.float32)
                     if turn == 0:
@@ -118,9 +122,12 @@
                         inside = (lane + WIDTH + EDGE - 2 * EDGE * turn) % WIDTH < 2 * EDGE
                         merged = jnp.where(inside, pltpu.roll(low, 2 * EDGE * turn, 1), merged)
                 out = jnp.dot(jnp.concatenate(highs, axis=1), weights, preferred_element_type=jnp.float32)
-                pltpu.store(packed, out[:, :WIDTH] + out[:, WIDTH:], mask=owner // 2 == first // 2 + pair)
+                pltpu.store(packed, out[:, :WIDTH] + out[:, WIDTH:], mask=owner // 2 == g * (size // 2) + first // 2 + pair)
             out = jnp.dot(merged.astype(jnp.bfloat16), lows, preferred_element_type=jnp.float32)
-            pltpu.store(small, out, mask=owner // 4 == first // 4)
+            pltpu.store(small, out, mask=owner // 4 == g * (size // 4) + first // 4)
+        return carry
+
+    lax.fori_loop(0, len(sizes), group, 0)
     lower = packed[: count // 2, :] + small[: count // 2, :]
     upper = packed[count // 2 :, :] + small[count // 2 :, :]
     lane = lane[: count // 2]
@@ -145,13 +152,10 @@
 
 def reach(values, weights):
     slot = lax.broadcasted_iota(jnp.int32, values.shape, 1) // 4
-    high = values.astype(jnp.bfloat16).astype(jnp.float32)
-    low = values - high
-    even = slot % 2 == 0
+    high, low = halves(values)
+    even = (slot % 2).astype(jnp.bfloat16) == 0
     highs = [jnp.where(even, high, pltpu.roll(high, 4, 1)), jnp.where(even, pltpu.roll(high, WIDTH - 4, 1), high)]
     lows = [pltpu.roll(low, 8, 1), pltpu.roll(low, 4, 1)]
-    highs = [x.astype(jnp.bfloat16) for x in highs]
-    lows = [x.astype(jnp.bfloat16) for x in lows]
     pair = (slot // 2).astype(jnp.bfloat16)
     slot = slot.astype(jnp.bfloat16)
     zero = jnp.zeros_like(lows[0])

time: 19.4 us -> 19.4 us (level)
  no operation moved by 1% of the time
where the time goes in v7:
time: 19.4 us; the launch traced here: 19.3 us
  starting transfers between devices  8.77 us (45%)
  Pallas kernels  8.73 us (45%)
  between operations  0.71 us (4%)
  waiting for transfers between devices  0.52 us (3%)
  other arithmetic  0.52 us (3%)
    ppermute x2, starting transfers between devices, local(): other = lax.ppermute(sums, 'lines', [(i, i ^ step) for i in range(across)])  4.69 us
    ppermute x1, starting transfers between devices, local(): outer = lax.ppermute(outer, 'blk', far + [(j, i) for i, j in far])  3.56 us
    pallas_call x1, Pallas kernels, local(): pl.pallas_call(functools.partial(edges_kernel, sizes), out_shape=(pltpu.V...  2.95 us
    pallas_call x2, Pallas kernels, flush(): pl.pallas_call(functools.partial(flush_kernel, start, size), out_shape=pl...  2.82 us
    pallas_call x1, Pallas kernels, local(): pl.pallas_call(near_kernel, out_shape=(pltpu.VMEM((rows, width), f32), pl...  2.11 us
    pallas_call x1, Pallas kernels, local(): pl.pallas_call(far_kernel, out_shape=(pltpu.VMEM((rows, width), f32), plt...  0.84 us
    ppermute x1, starting transfers between devices, local(): inner = lax.ppermute(inner, 'blk', [(i, i ^ 1) for i in range(blocks)])  0.52 us
    div x1, other arithmetic, local(): profile = sums.reshape(width) / (lines * across)  0.51 us
  transfers between devices with their start and end apart: 4, of which 2 were waited for; matrix products, arithmetic and copies ran while one was open for 0% of the time, Pallas kernels for 26%

profile of v7, /device:TPU:0, one launch (start us, length us, event | category | flops | bytes accessed | tf_op | source)
XLA Modules:
  0.0 19.3 jit_solution(15668398281169862151)
XLA Ops:
  0.6 0.0 copy-start
  0.6 0.0 copy-start.1
  0.7 0.0 copy-start.2
  0.7 3.0 %edges.1 = (f32[9216,128]{1,0:T(8,128)S(1)}, f32[144,128]{1,0:T(8,128)S(1)}, f32[144,128]{1,0:T(8,128)S(1)}) custom-call(f32[9216,128]{1,0:T(8,128)} %bitcast.7, bf16[128,256]{1,0:T(8,128)(2,1)} %constant.11.clone.weights_hbm, bf16[128,128]{1,0:T(8,128)(2,1)} %constant.12.clone.lows_hbm), custom_call_target="tpu_custom_call" | custom-call | tf_op jit(solution)/shard_map/edges/pallas_call | solution.py:217
  3.6 0.5 %collective-permute-start = (f32[144,128]{1,0:T(8,128)S(1)}, f32[144,128]{1,0:T(8,128)S(1)}, u32[]{:S(2)}, u32[]{:S(2)}) collective-permute-start(f32[144,128]{1,0:T(8,128)S(1)} %get-tuple-element.12), channel_id=1, source_target_pairs={{0,4},{4,0},{8,12},{12,8},{16,20},{20,16},{24,28},{28,24},{1,5},{5... | collective-permute-start | bytes 221192 | tf_op jit(solution)/shard_map/ppermute | solution.py:238
  4.1 3.6 %collective-permute-start.1 = (f32[144,128]{1,0:T(8,128)S(1)}, f32[144,128]{1,0:T(8,128)S(1)}, u32[]{:S(2)}, u32[]{:S(2)}) collective-permute-start(f32[144,128]{1,0:T(8,128)S(1)} %get-tuple-element.14), channel_id=1, source_target_pairs={{4,8},{12,16},{20,24},{28,0},{8,4},{16,12},{24,20},{0,28},{5,9},{1... | collective-permute-start | bytes 221192 | tf_op jit(solution)/shard_map/ppermute | solution.py:237
  7.7 0.0 collective-permute-done.inner_ref
  7.7 0.0 copy-done
  7.7 0.0 copy-done.1
  7.7 0.0 copy-done.2
  7.7 2.1 %near.1 = (f32[9216,128]{1,0:T(8,128)S(1)}, bf16[128,256]{1,0:T(8,128)(2,1)S(1)}) custom-call(f32[9216,128]{1,0:T(8,128)S(1)} %get-tuple-element.11.velocity_ref, f32[144,128]{1,0:T(8,128)S(1)} %collective-permute-done.inner_ref, bf16[128,256]{1,0:T(8,128)(2,1)S(1)} %copy-done, f32[4,128]{1,0:T(4,128)S(1)} %copy-done.1, f32[1,128]{1,0:T(1,128)S(1)} %bitcast.5), custom_call_target="tpu_custom_call" | custom-call | tf_op jit(solution)/shard_map/near/pallas_call | solution.py:239
  9.8 0.0 collective-permute-done.1.outer_ref
  9.8 0.8 %far.1 = (f32[9216,128]{1,0:T(8,128)S(1)}, f32[1,128]{1,0:T(1,128)S(1)}) custom-call(f32[9216,128]{1,0:T(8,128)S(1)} %get-tuple-element.13.solved_ref, f32[144,128]{1,0:T(8,128)S(1)} %collective-permute-done.1.outer_ref, bf16[128,256]{1,0:T(8,128)(2,1)S(1)} %get-tuple-element.15.weights_ref), custom_call_target="tpu_custom_call" | custom-call | tf_op jit(solution)/shard_map/far/pallas_call | solution.py:247
  10.7 1.9 %collective-permute-start.2 = (f32[1,128]{1,0:T(1,128)S(1)}, f32[1,128]{1,0:T(1,128)S(1)}, u32[]{:S(2)}, u32[]{:S(2)}) collective-permute-start(f32[1,128]{1,0:T(1,128)S(1)} %get-tuple-element.17), channel_id=1, source_target_pairs={{0,1},{1,0},{2,3},{3,2},{4,5},{5,4},{6,7},{7,6},{8,9},{9,8},{10,11... | collective-permute-start | bytes 1544 | tf_op jit(solution)/shard_map/ppermute | solution.py:272
  12.6 1.4 %flush.2.refs_0_ = f32[9216,128]{1,0:T(8,128)} custom-call(f32[9216,128]{1,0:T(8,128)S(1)} %get-tuple-element.16.values_ref), custom_call_target="tpu_custom_call" | custom-call | tf_op jit(solution)/shard_map/flush/pallas_call | solution.py:257
  14.0 0.3 %collective-permute-done.2 = f32[1,128]{1,0:T(1,128)S(1)} collective-permute-done((f32[1,128]{1,0:T(1,128)S(1)}, f32[1,128]{1,0:T(1,128)S(1)}, u32[]{:S(2)}, u32[]{:S(2)}) %collective-permute-start.2) | collective-permute-done | bytes 544 | tf_op jit(solution)/shard_map/ppermute | solution.py:272
  14.3 2.8 %collective-permute-start.3 = (f32[1,128]{1,0:T(1,128)S(1)}, f32[1,128]{1,0:T(1,128)S(1)}, u32[]{:S(2)}, u32[]{:S(2)}) collective-permute-start(f32[1,128]{1,0:T(1,128)S(1)} %add.6), channel_id=1, source_target_pairs={{0,2},{1,3},{2,0},{3,1},{4,6},{5,7},{6,4},{7,5},{8,10},{9,11},{10,... | collective-permute-start | bytes 1544 | tf_op jit(solution)/shard_map/ppermute | solution.py:272
  17.1 1.4 %flush.3 = f32[9216,128]{1,0:T(8,128)} custom-call(f32[9216,128]{1,0:T(8,128)S(1)} %get-tuple-element.16.values_ref, f32[9216,128]{1,0:T(8,128)} %flush.2.refs_0_), custom_call_target="tpu_custom_call", output_to_operand_aliasing={{}: (1, {})} | custom-call | tf_op jit(solution)/shard_map/flush/pallas_call | solution.py:257
  18.5 0.2 %collective-permute-done.3 = f32[1,128]{1,0:T(1,128)S(1)} collective-permute-done((f32[1,128]{1,0:T(1,128)S(1)}, f32[1,128]{1,0:T(1,128)S(1)}, u32[]{:S(2)}, u32[]{:S(2)}) %collective-permute-start.3) | collective-permute-done | bytes 544 | tf_op jit(solution)/shard_map/ppermute | solution.py:272
  18.7 0.5 %multiply_bitcast_fusion = f32[128]{0:T(128)} fusion(f32[1,128]{1,0:T(1,128)S(1)} %add.6, f32[1,128]{1,0:T(1,128)S(1)} %collective-permute-done.3), kind=kLoop, calls=%fused_computation | loop fusion | flops 256 | bytes 1536 | tf_op jit(solution)/shard_map/div | solution.py:280
  (1 shorter events, 0.0 us)
Async XLA Ops:
  0.6 7.1 %copy-start = (bf16[128,256]{1,0:T(8,128)(2,1)S(1)}, bf16[128,256]{1,0:T(8,128)(2,1)}, u32[]{:S(2)}) copy-start(bf16[128,256]{1,0:T(8,128)(2,1)} %constant.13.clone.weights_ref) | copy-start | bytes 196612
  0.6 7.1 %copy-start.1 = (f32[4,128]{1,0:T(4,128)S(1)}, f32[4,128]{1,0:T(4,128)}, u32[]{:S(2)}) copy-start(f32[4,128]{1,0:T(4,128)} %constant.14.clone.rows_ref) | copy-start | bytes 6148
  0.7 7.1 %copy-start.2 = (f32[128]{0:T(128)S(1)}, f32[128]{0:T(128)}, u32[]{:S(2)}) copy-start(f32[128]{0:T(128)} %param.7) | copy-start | bytes 1540
  3.6 4.1 %collective-permute-start = (f32[144,128]{1,0:T(8,128)S(1)}, f32[144,128]{1,0:T(8,128)S(1)}, u32[]{:S(2)}, u32[]{:S(2)}) collective-permute-start(f32[144,128]{1,0:T(8,128)S(1)} %get-tuple-element.12), channel_id=1, source_target_pairs={{0,4},{4,0},{8,12},{12,8},{16,20},{20,16},{24,28},{28,24},{1,5},{5... | collective-permute-start | bytes 221192 | tf_op jit(solution)/shard_map/ppermute | solution.py:238
  4.1 5.7 %collective-permute-start.1 = (f32[144,128]{1,0:T(8,128)S(1)}, f32[144,128]{1,0:T(8,128)S(1)}, u32[]{:S(2)}, u32[]{:S(2)}) collective-permute-start(f32[144,128]{1,0:T(8,128)S(1)} %get-tuple-element.14), channel_id=1, source_target_pairs={{4,8},{12,16},{20,24},{28,0},{8,4},{16,12},{24,20},{0,28},{5,9},{1... | collective-permute-start | bytes 221192 | tf_op jit(solution)/shard_map/ppermute | solution.py:237
  10.7 3.6 %collective-permute-start.2 = (f32[1,128]{1,0:T(1,128)S(1)}, f32[1,128]{1,0:T(1,128)S(1)}, u32[]{:S(2)}, u32[]{:S(2)}) collective-permute-start(f32[1,128]{1,0:T(1,128)S(1)} %get-tuple-element.17), channel_id=1, source_target_pairs={{0,1},{1,0},{2,3},{3,2},{4,5},{5,4},{6,7},{7,6},{8,9},{9,8},{10,11... | collective-permute-start | bytes 1544 | tf_op jit(solution)/shard_map/ppermute | solution.py:272
  14.3 4.4 %collective-permute-start.3 = (f32[1,128]{1,0:T(1,128)S(1)}, f32[1,128]{1,0:T(1,128)S(1)}, u32[]{:S(2)}, u32[]{:S(2)}) collective-permute-start(f32[1,128]{1,0:T(1,128)S(1)} %add.6), channel_id=1, source_target_pairs={{0,2},{1,3},{2,0},{3,1},{4,6},{5,7},{6,4},{7,5},{8,10},{9,11},{10,... | collective-permute-start | bytes 1544 | tf_op jit(solution)/shard_map/ppermute | solution.py:272

commit v8 on v7

--- a/solution.py
+++ b/solution.py
@@ -267,13 +267,13 @@
 
     derivs = flush(0, rows // 2)
     if across & (across - 1) == 0:
-        step = 1
-        while step < across:
+        step = across // 2
+        while step:
             other = lax.ppermute(sums, "lines", [(i, i ^ step) for i in range(across)])
-            if step == 1:
+            if step == across // 2:
                 other, derivs = lax.optimization_barrier((other, derivs))
             sums = sums + other
-            step *= 2
+            step //= 2
     else:
         sums = lax.psum(sums, "lines")
     derivs = flush(rows // 2, rows - rows // 2, derivs)

time: 19.4 us -> 19.4 us (level)
  no operation moved by 1% of the time
where the time goes in v8:
time: 19.4 us; the launch traced here: 19.3 us
  starting transfers between devices  8.77 us (45%)
  Pallas kernels  8.73 us (45%)
  between operations  0.71 us (4%)
  waiting for transfers between devices  0.52 us (3%)
  other arithmetic  0.52 us (3%)
    ppermute x2, starting transfers between devices, local(): other = lax.ppermute(sums, 'lines', [(i, i ^ step) for i in range(across)])  4.69 us
    ppermute x1, starting transfers between devices, local(): outer = lax.ppermute(outer, 'blk', far + [(j, i) for i, j in far])  3.56 us
    pallas_call x1, Pallas kernels, local(): pl.pallas_call(functools.partial(edges_kernel, sizes), out_shape=(pltpu.V...  2.95 us
    pallas_call x2, Pallas kernels, flush(): pl.pallas_call(functools.partial(flush_kernel, start, size), out_shape=pl...  2.82 us
    pallas_call x1, Pallas kernels, local(): pl.pallas_call(near_kernel, out_shape=(pltpu.VMEM((rows, width), f32), pl...  2.11 us
    pallas_call x1, Pallas kernels, local(): pl.pallas_call(far_kernel, out_shape=(pltpu.VMEM((rows, width), f32), plt...  0.84 us
    ppermute x1, starting transfers between devices, local(): inner = lax.ppermute(inner, 'blk', [(i, i ^ 1) for i in range(blocks)])  0.52 us
    div x1, other arithmetic, local(): profile = sums.reshape(width) / (lines * across)  0.51 us
  transfers between devices with their start and end apart: 4, of which 2 were waited for; matrix products, arithmetic and copies ran while one was open for 0% of the time, Pallas kernels for 26%

profile of v8, /device:TPU:0, one launch (start us, length us, event | category | flops | bytes accessed | tf_op | source)
XLA Modules:
  0.0 19.3 jit_solution(3029861870026698469)
XLA Ops:
  0.6 0.0 copy-start
  0.6 0.0 copy-start.1
  0.7 0.0 copy-start.2
  0.7 3.0 %edges.1 = (f32[9216,128]{1,0:T(8,128)S(1)}, f32[144,128]{1,0:T(8,128)S(1)}, f32[144,128]{1,0:T(8,128)S(1)}) custom-call(f32[9216,128]{1,0:T(8,128)} %bitcast.7, bf16[128,256]{1,0:T(8,128)(2,1)} %constant.11.clone.weights_hbm, bf16[128,128]{1,0:T(8,128)(2,1)} %constant.12.clone.lows_hbm), custom_call_target="tpu_custom_call" | custom-call | tf_op jit(solution)/shard_map/edges/pallas_call | solution.py:217
  3.6 0.5 %collective-permute-start = (f32[144,128]{1,0:T(8,128)S(1)}, f32[144,128]{1,0:T(8,128)S(1)}, u32[]{:S(2)}, u32[]{:S(2)}) collective-permute-start(f32[144,128]{1,0:T(8,128)S(1)} %get-tuple-element.12), channel_id=1, source_target_pairs={{0,4},{4,0},{8,12},{12,8},{16,20},{20,16},{24,28},{28,24},{1,5},{5... | collective-permute-start | bytes 221192 | tf_op jit(solution)/shard_map/ppermute | solution.py:238
  4.1 3.6 %collective-permute-start.1 = (f32[144,128]{1,0:T(8,128)S(1)}, f32[144,128]{1,0:T(8,128)S(1)}, u32[]{:S(2)}, u32[]{:S(2)}) collective-permute-start(f32[144,128]{1,0:T(8,128)S(1)} %get-tuple-element.14), channel_id=1, source_target_pairs={{4,8},{12,16},{20,24},{28,0},{8,4},{16,12},{24,20},{0,28},{5,9},{1... | collective-permute-start | bytes 221192 | tf_op jit(solution)/shard_map/ppermute | solution.py:237
  7.7 0.0 collective-permute-done.inner_ref
  7.7 0.0 copy-done
  7.7 0.0 copy-done.1
  7.7 0.0 copy-done.2
  7.7 2.1 %near.1 = (f32[9216,128]{1,0:T(8,128)S(1)}, bf16[128,256]{1,0:T(8,128)(2,1)S(1)}) custom-call(f32[9216,128]{1,0:T(8,128)S(1)} %get-tuple-element.11.velocity_ref, f32[144,128]{1,0:T(8,128)S(1)} %collective-permute-done.inner_ref, bf16[128,256]{1,0:T(8,128)(2,1)S(1)} %copy-done, f32[4,128]{1,0:T(4,128)S(1)} %copy-done.1, f32[1,128]{1,0:T(1,128)S(1)} %bitcast.5), custom_call_target="tpu_custom_call" | custom-call | tf_op jit(solution)/shard_map/near/pallas_call | solution.py:239
  9.8 0.0 collective-permute-done.1.outer_ref
  9.8 0.8 %far.1 = (f32[9216,128]{1,0:T(8,128)S(1)}, f32[1,128]{1,0:T(1,128)S(1)}) custom-call(f32[9216,128]{1,0:T(8,128)S(1)} %get-tuple-element.13.solved_ref, f32[144,128]{1,0:T(8,128)S(1)} %collective-permute-done.1.outer_ref, bf16[128,256]{1,0:T(8,128)(2,1)S(1)} %get-tuple-element.15.weights_ref), custom_call_target="tpu_custom_call" | custom-call | tf_op jit(solution)/shard_map/far/pallas_call | solution.py:247
  10.7 2.9 %collective-permute-start.2 = (f32[1,128]{1,0:T(1,128)S(1)}, f32[1,128]{1,0:T(1,128)S(1)}, u32[]{:S(2)}, u32[]{:S(2)}) collective-permute-start(f32[1,128]{1,0:T(1,128)S(1)} %get-tuple-element.17), channel_id=1, source_target_pairs={{0,2},{1,3},{2,0},{3,1},{4,6},{5,7},{6,4},{7,5},{8,10},{9,11},{10,... | collective-permute-start | bytes 1544 | tf_op jit(solution)/shard_map/ppermute | solution.py:272
  13.6 1.4 %flush.2.refs_0_ = f32[9216,128]{1,0:T(8,128)} custom-call(f32[9216,128]{1,0:T(8,128)S(1)} %get-tuple-element.16.values_ref), custom_call_target="tpu_custom_call" | custom-call | tf_op jit(solution)/shard_map/flush/pallas_call | solution.py:257
  15.0 0.2 %collective-permute-done.2 = f32[1,128]{1,0:T(1,128)S(1)} collective-permute-done((f32[1,128]{1,0:T(1,128)S(1)}, f32[1,128]{1,0:T(1,128)S(1)}, u32[]{:S(2)}, u32[]{:S(2)}) %collective-permute-start.2) | collective-permute-done | bytes 544 | tf_op jit(solution)/shard_map/ppermute | solution.py:272
  15.2 1.8 %collective-permute-start.3 = (f32[1,128]{1,0:T(1,128)S(1)}, f32[1,128]{1,0:T(1,128)S(1)}, u32[]{:S(2)}, u32[]{:S(2)}) collective-permute-start(f32[1,128]{1,0:T(1,128)S(1)} %add.6), channel_id=1, source_target_pairs={{0,1},{1,0},{2,3},{3,2},{4,5},{5,4},{6,7},{7,6},{8,9},{9,8},{10,11... | collective-permute-start | bytes 1544 | tf_op jit(solution)/shard_map/ppermute | solution.py:272
  17.0 1.4 %flush.3 = f32[9216,128]{1,0:T(8,128)} custom-call(f32[9216,128]{1,0:T(8,128)S(1)} %get-tuple-element.16.values_ref, f32[9216,128]{1,0:T(8,128)} %flush.2.refs_0_), custom_call_target="tpu_custom_call", output_to_operand_aliasing={{}: (1, {})} | custom-call | tf_op jit(solution)/shard_map/flush/pallas_call | solution.py:257
  18.4 0.3 %collective-permute-done.3 = f32[1,128]{1,0:T(1,128)S(1)} collective-permute-done((f32[1,128]{1,0:T(1,128)S(1)}, f32[1,128]{1,0:T(1,128)S(1)}, u32[]{:S(2)}, u32[]{:S(2)}) %collective-permute-start.3) | collective-permute-done | bytes 544 | tf_op jit(solution)/shard_map/ppermute | solution.py:272
  18.7 0.5 %multiply_bitcast_fusion = f32[128]{0:T(128)} fusion(f32[1,128]{1,0:T(1,128)S(1)} %add.6, f32[1,128]{1,0:T(1,128)S(1)} %collective-permute-done.3), kind=kLoop, calls=%fused_computation | loop fusion | flops 256 | bytes 1536 | tf_op jit(solution)/shard_map/div | solution.py:280
  (1 shorter events, 0.0 us)
Async XLA Ops:
  0.6 7.1 %copy-start = (bf16[128,256]{1,0:T(8,128)(2,1)S(1)}, bf16[128,256]{1,0:T(8,128)(2,1)}, u32[]{:S(2)}) copy-start(bf16[128,256]{1,0:T(8,128)(2,1)} %constant.13.clone.weights_ref) | copy-start | bytes 196612
  0.6 7.1 %copy-start.1 = (f32[4,128]{1,0:T(4,128)S(1)}, f32[4,128]{1,0:T(4,128)}, u32[]{:S(2)}) copy-start(f32[4,128]{1,0:T(4,128)} %constant.14.clone.rows_ref) | copy-start | bytes 6148
  0.7 7.1 %copy-start.2 = (f32[128]{0:T(128)S(1)}, f32[128]{0:T(128)}, u32[]{:S(2)}) copy-start(f32[128]{0:T(128)} %param.7) | copy-start | bytes 1540
  3.6 4.1 %collective-permute-start = (f32[144,128]{1,0:T(8,128)S(1)}, f32[144,128]{1,0:T(8,128)S(1)}, u32[]{:S(2)}, u32[]{:S(2)}) collective-permute-start(f32[144,128]{1,0:T(8,128)S(1)} %get-tuple-element.12), channel_id=1, source_target_pairs={{0,4},{4,0},{8,12},{12,8},{16,20},{20,16},{24,28},{28,24},{1,5},{5... | collective-permute-start | bytes 221192 | tf_op jit(solution)/shard_map/ppermute | solution.py:238
  4.1 5.7 %collective-permute-start.1 = (f32[144,128]{1,0:T(8,128)S(1)}, f32[144,128]{1,0:T(8,128)S(1)}, u32[]{:S(2)}, u32[]{:S(2)}) collective-permute-start(f32[144,128]{1,0:T(8,128)S(1)} %get-tuple-element.14), channel_id=1, source_target_pairs={{4,8},{12,16},{20,24},{28,0},{8,4},{16,12},{24,20},{0,28},{5,9},{1... | collective-permute-start | bytes 221192 | tf_op jit(solution)/shard_map/ppermute | solution.py:237
  10.7 4.5 %collective-permute-start.2 = (f32[1,128]{1,0:T(1,128)S(1)}, f32[1,128]{1,0:T(1,128)S(1)}, u32[]{:S(2)}, u32[]{:S(2)}) collective-permute-start(f32[1,128]{1,0:T(1,128)S(1)} %get-tuple-element.17), channel_id=1, source_target_pairs={{0,2},{1,3},{2,0},{3,1},{4,6},{5,7},{6,4},{7,5},{8,10},{9,11},{10,... | collective-permute-start | bytes 1544 | tf_op jit(solution)/shard_map/ppermute | solution.py:272
  15.2 3.5 %collective-permute-start.3 = (f32[1,128]{1,0:T(1,128)S(1)}, f32[1,128]{1,0:T(1,128)S(1)}, u32[]{:S(2)}, u32[]{:S(2)}) collective-permute-start(f32[1,128]{1,0:T(1,128)S(1)} %add.6), channel_id=1, source_target_pairs={{0,1},{1,0},{2,3},{3,2},{4,5},{5,4},{6,7},{7,6},{8,9},{9,8},{10,11... | collective-permute-start | bytes 1544 | tf_op jit(solution)/shard_map/ppermute | solution.py:272
